TPU v7x, 32 devices: a whole 2x2x4 slice. The times are simulated.
32 devices in a mesh: dp: 4 (over y, x), expert: 8 (over z, core).
Axes of the slice: x: 2, y: 2, z: 4, core: 2. Of those that a mesh axis runs over, the one named last changes fastest.
Arguments:
- tokens: bfloat16 [256, 4096], P('expert', 'dp'), may hold values from -6 to 6
- cotangent: bfloat16 [256, 4096], P('expert', 'dp'), may hold values from -6 to 6
- expert_ids: int32 [256, 3], P('expert'), may hold values from 0 to 5, all different within a row; in each aligned block of 32 rows (0 to 31, 32 to 63, ...) at most 16 rows name the same one
- gate_weights: float32 [256, 3], P('expert'), may hold values from 0.2 to 1
- slot_table: int32 [8], replicated, may hold values from 0 to 5, as said below
- split_count: int32 [6], replicated, may hold values from 0 to 8
- w_gate: bfloat16 [8, 4096, 768], P('expert', 'dp'), may hold values from -0.09375 to 0.09375
- w_up: bfloat16 [8, 4096, 768], P('expert', 'dp'), may hold values from -0.09375 to 0.09375
- w_down: bfloat16 [8, 768, 4096], P('expert', None, 'dp'), may hold values from -0.21875 to 0.21875
Outputs:
- mixed: bfloat16 [256, 4096], P('expert', 'dp')
- token_grad: bfloat16 [256, 4096], P('expert', 'dp')
- gate_grad: bfloat16 [8, 4096, 768], P('expert', 'dp')
- up_grad: bfloat16 [8, 4096, 768], P('expert', 'dp')
- down_grad: bfloat16 [8, 768, 4096], P('expert', None, 'dp')
Inputs may be any that keep to these rules, and one draw needn't show every extreme that they name: `expert_ids`: in the rows of one device (aligned blocks of 32 rows), no expert is named more than 16 times. `slot_table`: every expert is held by one or two slots; exactly 2 experts are held by two, and those sit on slots s and s + 4 with s below 4.
All inputs are finite; a program needn't handle non-finite values.
Results may differ from a plain program's by a relative error of at most 0.028.
Values may be sent and summed in bfloat16 or wider, within the bound.
No kernel may reach another device: no remote copies, remote signals or barrier semaphores. Data moves between devices by JAX's collectives and lax.ppermute only.
A program may use at most 64 MiB of HBM per device.

v0:
```python
import jax
import jax.numpy as jnp
from jax import lax
from jax.sharding import PartitionSpec as P


def shifted(value, axis, steps):
    count = lax.axis_size(axis)
    pairs = [(source, (source + steps) % count) for source in range(count)]
    return lax.ppermute(value, axis, pairs)


def slot_choice(expert_ids, slot_table, split_count, source):
    slot_count = slot_table.shape[0]
    expert_count = split_count.shape[0]
    slot_iota = jnp.arange(slot_count, dtype=jnp.int32)
    expert_iota = jnp.arange(expert_count, dtype=jnp.int32)
    holds = slot_table[None, :] == expert_iota[:, None]
    lower = jnp.min(jnp.where(holds, slot_iota[None, :], slot_count), axis=1)
    upper = jnp.max(jnp.where(holds, slot_iota[None, :], -1), axis=1)
    chosen = jnp.where(source < split_count, lower, upper)
    flat_ids = expert_ids.reshape(-1)
    matches = flat_ids[:, None] == expert_iota[None, :]
    target = jnp.sum(jnp.where(matches, chosen[None, :], 0), axis=1)
    onehot = (target[:, None] == slot_iota[None, :]).astype(jnp.int32)
    before = jnp.cumsum(onehot, axis=0) - onehot
    position = jnp.sum(before * onehot, axis=1)
    return (target, position)


def swiglu(gate_pre, up_pre):
    return (jax.nn.silu(gate_pre) * up_pre).astype(jnp.bfloat16)


def swiglu_back(gate_pre, up_pre, upstream):
    sigma = jax.nn.sigmoid(gate_pre)
    gate_back = upstream * up_pre * sigma * (1.0 + gate_pre * (1.0 - sigma))
    up_back = upstream * gate_pre * sigma
    return (gate_back.astype(jnp.bfloat16), up_back.astype(jnp.bfloat16))


def row_contract(left, right_mat):
    return lax.dot_general(
        left, right_mat, (((0,), (0,)), ((), ())), preferred_element_type=jnp.float32
    )


def col_contract(left, right_mat):
    return lax.dot_general(
        left, right_mat, (((1,), (1,)), ((), ())), preferred_element_type=jnp.float32
    )


def on_device(
    tokens, cotangent, expert_ids, gate_weights, slot_table, split_count, w_gate, w_up, w_down
):
    slot_count = slot_table.shape[0]
    expert_count = split_count.shape[0]
    token_count, top_k = expert_ids.shape
    shard_width = tokens.shape[1]
    capacity = max(2, (token_count * top_k + expert_count - 1) // expert_count)
    source = lax.axis_index("expert")
    target, position = slot_choice(expert_ids, slot_table, split_count, source)
    destination = target * capacity + position
    slot_iota = jnp.arange(slot_count * capacity, dtype=jnp.int32)
    selector = (slot_iota[:, None] == destination[None, :]).astype(jnp.bfloat16)
    per_token = jnp.sum(selector.reshape(slot_count * capacity, token_count, top_k), axis=2)
    send_rows = jnp.dot(per_token, tokens, preferred_element_type=jnp.float32).astype(jnp.bfloat16)
    scaled = (gate_weights[:, :, None] * cotangent[:, None, :].astype(jnp.float32)).astype(
        jnp.bfloat16
    )
    send_back = jnp.dot(
        selector,
        scaled.reshape(token_count * top_k, shard_width),
        preferred_element_type=jnp.float32,
    ).astype(jnp.bfloat16)
    got_rows, got_back = (
        lax.all_to_all(
            send_rows.reshape(slot_count, capacity, shard_width),
            "expert",
            split_axis=0,
            concat_axis=0,
            tiled=True,
        ),
        lax.all_to_all(
            send_back.reshape(slot_count, capacity, shard_width),
            "expert",
            split_axis=0,
            concat_axis=0,
            tiled=True,
        ),
    )
    slot_in = got_rows.reshape(-1, shard_width)
    slot_back = got_back.reshape(-1, shard_width)
    gate_mat = w_gate[0]
    up_mat = w_up[0]
    down_mat = w_down[0]
    gate_part = jnp.dot(slot_in, gate_mat, preferred_element_type=jnp.float32)
    up_part = jnp.dot(slot_in, up_mat, preferred_element_type=jnp.float32)
    gate_pre, up_pre = (
        lax.psum(gate_part.astype(jnp.bfloat16), "dp").astype(jnp.float32),
        lax.psum(up_part.astype(jnp.bfloat16), "dp").astype(jnp.float32),
    )
    hidden_act = swiglu(gate_pre, up_pre)
    slot_out = jnp.dot(hidden_act, down_mat, preferred_element_type=jnp.float32).astype(
        jnp.bfloat16
    )
    upstream = lax.psum(col_contract(slot_back, down_mat).astype(jnp.bfloat16), "dp").astype(
        jnp.float32
    )
    gate_back, up_back = swiglu_back(gate_pre, up_pre, upstream)
    grad_gate = row_contract(slot_in, gate_back).astype(jnp.bfloat16)
    grad_up = row_contract(slot_in, up_back).astype(jnp.bfloat16)
    grad_down = row_contract(hidden_act, slot_back).astype(jnp.bfloat16)
    slot_dx = (col_contract(gate_back, gate_mat) + col_contract(up_back, up_mat)).astype(
        jnp.bfloat16
    )
    out_back, dx_back = (
        lax.all_to_all(
            slot_out.reshape(slot_count, capacity, shard_width),
            "expert",
            split_axis=0,
            concat_axis=0,
            tiled=True,
        ),
        lax.all_to_all(
            slot_dx.reshape(slot_count, capacity, shard_width),
            "expert",
            split_axis=0,
            concat_axis=0,
            tiled=True,
        ),
    )
    out_assign = row_contract(selector, out_back.reshape(-1, shard_width)).reshape(
        token_count, top_k, shard_width
    )
    dx_assign = row_contract(selector, dx_back.reshape(-1, shard_width)).reshape(
        token_count, top_k, shard_width
    )
    mixed = jnp.sum(gate_weights[:, :, None] * out_assign, axis=1).astype(jnp.bfloat16)
    token_grad = jnp.sum(dx_assign, axis=1).astype(jnp.bfloat16)
    half_axis = lax.axis_size("expert") // 2
    own_expert = lax.dynamic_index_in_dim(slot_table, source, 0, keepdims=False)
    partner_slot = (source + half_axis) % slot_count
    partner_expert = lax.dynamic_index_in_dim(slot_table, partner_slot, 0, keepdims=False)
    paired = (own_expert == partner_expert).astype(jnp.float32)
    far_in, far_back, far_act, far_gback, far_uback = shifted(
        (slot_in, slot_back, hidden_act, gate_back, up_back), "expert", half_axis
    )
    far_gate = row_contract(far_in, far_gback).astype(jnp.bfloat16)
    far_up = row_contract(far_in, far_uback).astype(jnp.bfloat16)
    far_down = row_contract(far_act, far_back).astype(jnp.bfloat16)
    gate_grad = (grad_gate.astype(jnp.float32) + paired * far_gate.astype(jnp.float32)).astype(
        jnp.bfloat16
    )[None]
    up_grad = (grad_up.astype(jnp.float32) + paired * far_up.astype(jnp.float32)).astype(
        jnp.bfloat16
    )[None]
    down_grad = (grad_down.astype(jnp.float32) + paired * far_down.astype(jnp.float32)).astype(
        jnp.bfloat16
    )[None]
    return (mixed, token_grad, gate_grad, up_grad, down_grad)


def solution(mesh):
    return jax.shard_map(
        on_device,
        mesh=mesh,
        in_specs=(
            P("expert", "dp"),
            P("expert", "dp"),
            P("expert", None),
            P("expert", None),
            P(),
            P(),
            P("expert", "dp", None),
            P("expert", "dp", None),
            P("expert", None, "dp"),
        ),
        out_specs=(
            P("expert", "dp"),
            P("expert", "dp"),
            P("expert", "dp", None),
            P("expert", "dp", None),
            P("expert", None, "dp"),
        ),
        check_vma=False,
    )
```

profile of v0, /device:TPU:0, one launch (start us, length us, event | category | flops | bytes accessed | tf_op | source)
XLA Modules:
  0.0 147.4 jit_solution(9655682628774225093)
XLA Ops:
  7.2 0.0 copy-start
  7.2 0.0 copy-start.5
  7.2 0.9 select_reduce_fusion.2
  8.1 0.8 copy.20
  8.9 0.1 eq.86
  9.0 0.7 compare_select_fusion
  9.7 0.1 select_reduce_fusion.1
  9.7 0.1 fusion.45
  9.8 0.1 reduce_window_sum.11
  10.0 0.2 select_reduce_fusion
  10.2 0.1 add.52
  10.3 0.1 copy.21
  10.3 0.1 fusion.50
  10.4 1.8 %convolution_convert_fusion.6 = bf16[128,1024]{1,0:T(8,128)(2,1)} fusion(bf16[128,32]{0,1:T(8,128)(2,1)S(1)} %fusion.50, bf16[32,1024]{1,0:T(8,128)(2,1)} %param.9), kind=kOutput, calls=%fused_computation.25 | convolution fusion | flops 8519680 | bytes 335872 | tf_op jit(solution)/shard_map/dot_general | solution.py:68
  12.2 6.4 %all-to-all-start = ((bf16[8,16,1024]{2,1,0:T(8,128)(2,1)}), bf16[8,16,1024]{2,1,0:T(8,128)(2,1)S(1)}, u32[]{:S(2)}, u32[]{:S(2)}) async-start(bf16[8,16,1024]{2,1,0:T(8,128)(2,1)} %bitcast), calls=%async_computation | async-start | bytes 524288 | tf_op jit(solution)/shard_map/all_to_all | solution.py:78
  18.6 1.0 mul.91
  19.6 0.9 mul.92
  20.5 0.0 copy-done.5
  20.5 0.1 copy.23
  20.6 0.1 mul.89
  20.7 0.0 copy-start.1
  20.7 2.1 %convolution_convert_fusion.7 = bf16[128,1024]{1,0:T(8,128)(2,1)} fusion(f32[96,1024]{1,0:T(8,128)} %mul.92, f32[96]{0:T(128)S(1)} %mul.89, s32[96]{0:T(128)S(1)} %multiply_add_fusion), kind=kOutput, calls=%fused_computation.28 | convolution fusion | flops 25505792 | bytes 656128 | tf_op jit(solution)/shard_map/dot_general | solution.py:72
  22.8 5.5 %all-to-all-done = bf16[8,16,1024]{2,1,0:T(8,128)(2,1)S(1)} async-done(((bf16[8,16,1024]{2,1,0:T(8,128)(2,1)}), bf16[8,16,1024]{2,1,0:T(8,128)(2,1)S(1)}, u32[]{:S(2)}, u32[]{:S(2)}) %all-to-all-start) | async-done | bytes 262176 | tf_op jit(solution)/shard_map/all_to_all | solution.py:78
  28.3 4.0 %all-to-all-start.2 = ((bf16[8,16,1024]{2,1,0:T(8,128)(2,1)}), bf16[8,16,1024]{2,1,0:T(8,128)(2,1)}, u32[]{:S(2)}, u32[]{:S(2)}) async-start(bf16[8,16,1024]{2,1,0:T(8,128)(2,1)} %bitcast.73), calls=%async_computation.2 | async-start | bytes 524288 | tf_op jit(solution)/shard_map/all_to_all | solution.py:85
  32.4 0.0 all-reduce.3.cloned.1.call-start
  32.4 0.0 copy-done
  32.4 1.1 fusion.27
  33.5 0.0 copy-done.1
  33.5 1.1 fusion.24
  34.5 7.5 %all-to-all-done.2 = bf16[8,16,1024]{2,1,0:T(8,128)(2,1)} async-done(((bf16[8,16,1024]{2,1,0:T(8,128)(2,1)}), bf16[8,16,1024]{2,1,0:T(8,128)(2,1)}, u32[]{:S(2)}, u32[]{:S(2)}) %all-to-all-start.2) | async-done | bytes 262176 | tf_op jit(solution)/shard_map/all_to_all | solution.py:85
  42.1 2.8 %fusion.30 = bf16[128,768]{1,0:T(8,128)(2,1)} fusion(bf16[128,1024]{1,0:T(8,128)(2,1)} %bitcast.9, bf16[1,768,1024]{2,1,0:T(8,128)(2,1)} %param.17), kind=kOutput, calls=%fused_computation.32 | convolution fusion | flops 201424896 | bytes 2031616 | tf_op jit(solution)/shard_map/dot_general | solution.py:49
  44.9 0.0 all-reduce.3.cloned.1.call-update
  44.9 0.1 iota_compare_fusion.4
  45.1 0.0 copy-done.6
  45.1 0.6 fusion.51
  47.0 0.1 collective-permute-start
  47.1 2.9 %collective-permute-start.4 = (bf16[128,1024]{1,0:T(8,128)(2,1)}, bf16[128,1024]{1,0:T(8,128)(2,1)}, u32[]{:S(2)}, u32[]{:S(2)}) collective-permute-start(bf16[128,1024]{1,0:T(8,128)(2,1)} %bitcast.9), channel_id=1, source_target_pairs={{0,4},{1,5},{2,6},{3,7},{4,0},{5,1},{6,2},{7,3},{8,12},{9,13},{10,... | collective-permute-start | bytes 786440 | tf_op jit(solution)/shard_map/ppermute | solution.py:10
  50.0 40.5 %all-reduce.3.cloned.1.call-done = (bf16[128,768]{1,0:T(8,128)(2,1)}, bf16[128,768]{1,0:T(8,128)(2,1)}, bf16[128,768]{1,0:T(8,128)(2,1)}) async-done(((bf16[128,768]{1,0:T(8,128)(2,1)}, bf16[128,768]{1,0:T(8,128)(2,1)}, bf16[128,768]{1,0:T(8,128)(2,1)}), (bf16[128,768]{1,0:T(8,128)(2,1)}, bf16[128,768]{1,0:T(8,128)(2,1)}, bf16[128,768]{1,0:T(8,128)(2,1)})) %all-reduce.3.cloned.1.call-update) | async-done | bytes 589840 | tf_op jit(solution)/shard_map/psum | solution.py:102
  90.4 2.1 %fusion.37 = (bf16[128,768]{1,0:T(8,128)(2,1)}, bf16[128,768]{1,0:T(8,128)(2,1)}, bf16[128,768]{1,0:T(8,128)(2,1)}) fusion(bf16[128,768]{1,0:T(8,128)(2,1)} %get-tuple-element.7, bf16[128,768]{1,0:T(8,128)(2,1)} %get-tuple-element.9, bf16[128,768]{1,0:T(8,128)(2,1)} %get-tuple-element.8), kind=kLoop, calls=%fused_computation.44 | loop fusion | flops 1867776 | bytes 1179648 | tf_op jit(solution)/shard_map/convert_element_type | solution.py:39
  92.6 2.7 %convolution_convert_fusion.5 = bf16[1024,768]{1,0:T(8,128)(2,1)} fusion(bf16[128,1024]{1,0:T(8,128)(2,1)S(1)} %bitcast.71, bf16[128,768]{1,0:T(8,128)(2,1)} %get-tuple-element.10), kind=kOutput, calls=%fused_computation.8 | convolution fusion | flops 202113024 | bytes 2031616 | tf_op jit(solution)/shard_map/dot_general | solution.py:43
  95.2 2.4 %collective-permute-start.1 = (bf16[128,768]{1,0:T(8,128)(2,1)}, bf16[128,768]{1,0:T(8,128)(2,1)}, u32[]{:S(2)}, u32[]{:S(2)}) collective-permute-start(bf16[128,768]{1,0:T(8,128)(2,1)} %get-tuple-element.10), channel_id=1, source_target_pairs={{0,4},{1,5},{2,6},{3,7},{4,0},{5,1},{6,2},{7,3},{8,12},{9,13},{10,... | collective-permute-start | bytes 589832 | tf_op jit(solution)/shard_map/ppermute | solution.py:10
  97.6 2.4 %fusion.7 = f32[128,1024]{1,0:T(8,128)} fusion(bf16[128,768]{1,0:T(8,128)(2,1)} %get-tuple-element.11, bf16[1,1024,768]{2,1,0:T(8,128)(2,1)S(1)} %copy-done), kind=kOutput, calls=%fused_computation.16 | convolution fusion | flops 201326592 | bytes 2293760 | tf_op jit(solution)/shard_map/dot_general | solution.py:49
  100.0 2.8 %convolution_convert_fusion.3 = bf16[1024,768]{1,0:T(8,128)(2,1)} fusion(bf16[128,1024]{1,0:T(8,128)(2,1)S(1)} %bitcast.72, bf16[128,768]{1,0:T(8,128)(2,1)} %get-tuple-element.11), kind=kOutput, calls=%fused_computation.6 | convolution fusion | flops 202113024 | bytes 2031616 | tf_op jit(solution)/shard_map/dot_general | solution.py:43
  102.8 0.5 collective-permute-start.2
  103.3 0.0 copy-done.2
  103.3 2.0 %fusion.21 = bf16[128,1024]{1,0:T(8,128)(2,1)} fusion(bf16[128,768]{1,0:T(8,128)(2,1)} %get-tuple-element.12, bf16[1,768,1024]{2,1,0:T(8,128)(2,1)S(1)} %copy-done.2), kind=kOutput, calls=%fused_computation.27 | convolution fusion | flops 201457664 | bytes 2031616 | tf_op jit(solution)/shard_map/dot_general | solution.py:105
  105.3 4.6 %all-to-all-start.1 = ((bf16[8,16,1024]{2,1,0:T(8,128)(2,1)}), bf16[8,16,1024]{2,1,0:T(8,128)(2,1)}, u32[]{:S(2)}, u32[]{:S(2)}) async-start(bf16[8,16,1024]{2,1,0:T(8,128)(2,1)} %bitcast.75), calls=%async_computation.1 | async-start | bytes 524288 | tf_op jit(solution)/shard_map/all_to_all | solution.py:119
  109.9 2.5 %fusion.18 = bf16[128,1024]{1,0:T(8,128)(2,1)} fusion(f32[128,1024]{1,0:T(8,128)} %fusion.7, bf16[128,768]{1,0:T(8,128)(2,1)} %get-tuple-element.10, bf16[1,1024,768]{2,1,0:T(8,128)(2,1)S(1)} %copy-done.1), kind=kOutput, calls=%fused_computation.26 | convolution fusion | flops 201588736 | bytes 2555904 | tf_op jit(solution)/shard_map/dot_general | solution.py:49
  112.4 2.9 %convolution_convert_fusion.1 = bf16[768,1024]{1,0:T(8,128)(2,1)} fusion(bf16[128,768]{1,0:T(8,128)(2,1)} %get-tuple-element.12, bf16[128,1024]{1,0:T(8,128)(2,1)} %bitcast.9), kind=kOutput, calls=%fused_computation.4 | convolution fusion | flops 202113024 | bytes 2031616 | tf_op jit(solution)/shard_map/dot_general | solution.py:43
  115.4 2.9 %collective-permute-start.3 = (bf16[128,768]{1,0:T(8,128)(2,1)}, bf16[128,768]{1,0:T(8,128)(2,1)}, u32[]{:S(2)}, u32[]{:S(2)}) collective-permute-start(bf16[128,768]{1,0:T(8,128)(2,1)} %get-tuple-element.12), channel_id=1, source_target_pairs={{0,4},{1,5},{2,6},{3,7},{4,0},{5,1},{6,2},{7,3},{8,12},{9,13},{10,... | collective-permute-start | bytes 589832 | tf_op jit(solution)/shard_map/ppermute | solution.py:10
  118.3 0.0 collective-permute-done
  118.3 0.0 collective-permute-done.1
  118.3 2.8 %fusion = bf16[1,1024,768]{2,1,0:T(8,128)(2,1)} fusion(bf16[1024,768]{1,0:T(8,128)(2,1)S(1)} %copy-done.4, f32[]{:T(128)} %bitcast.13, bf16[128,1024]{1,0:T(8,128)(2,1)} %collective-permute-done, bf16[128,768]{1,0:T(8,128)(2,1)} %collective-permute-done.1), kind=kOutput, calls=%fused_computation.9 | convolution fusion | flops 206045184 | bytes 3604484 | tf_op jit(solution)/shard_map/dot_general | solution.py:43
  121.0 5.3 %all-to-all-done.1 = bf16[8,16,1024]{2,1,0:T(8,128)(2,1)} async-done(((bf16[8,16,1024]{2,1,0:T(8,128)(2,1)}), bf16[8,16,1024]{2,1,0:T(8,128)(2,1)}, u32[]{:S(2)}, u32[]{:S(2)}) %all-to-all-start.1) | async-done | bytes 262176 | tf_op jit(solution)/shard_map/all_to_all | solution.py:119
  126.4 3.7 %all-to-all-start.3 = ((bf16[8,16,1024]{2,1,0:T(8,128)(2,1)}), bf16[8,16,1024]{2,1,0:T(8,128)(2,1)S(1)}, u32[]{:S(2)}, u32[]{:S(2)}) async-start(bf16[8,16,1024]{2,1,0:T(8,128)(2,1)} %bitcast.10), calls=%async_computation.3 | async-start | bytes 524288 | tf_op jit(solution)/shard_map/all_to_all | solution.py:126
  130.0 0.0 collective-permute-done.4
  130.0 0.0 collective-permute-done.3
  130.1 3.4 %fusion.2 = bf16[1,768,1024]{2,1,0:T(8,128)(2,1)} fusion(bf16[768,1024]{1,0:T(8,128)(2,1)} %convolution_convert_fusion.1, f32[]{:T(128)} %bitcast.13, bf16[128,768]{1,0:T(8,128)(2,1)} %collective-permute-done.3, bf16[128,1024]{1,0:T(8,128)(2,1)} %collective-permute-done.4), kind=kOutput, calls=%fused_computation.11 | convolution fusion | flops 206045184 | bytes 3604484 | tf_op jit(solution)/shard_map/dot_general | solution.py:43
  133.5 0.0 collective-permute-done.2
  133.5 0.0 copy-done.3
  133.5 2.8 %fusion.1 = bf16[1,1024,768]{2,1,0:T(8,128)(2,1)} fusion(bf16[1024,768]{1,0:T(8,128)(2,1)S(1)} %copy-done.3, f32[]{:T(128)} %bitcast.13, bf16[128,1024]{1,0:T(8,128)(2,1)} %collective-permute-done, bf16[128,768]{1,0:T(8,128)(2,1)} %collective-permute-done.2), kind=kOutput, calls=%fused_computation.10 | convolution fusion | flops 206045184 | bytes 3604484 | tf_op jit(solution)/shard_map/dot_general | solution.py:43
  136.2 1.8 %fusion.33 = bf16[32,1024]{1,0:T(8,128)(2,1)} fusion(bf16[128,1024,1]{1,0,2:T(8,128)(2,1)} %bitcast.7, f32[32,3]{0,1:T(4,128)S(1)} %copy-done.5, pred[32,3,128]{2,1,0:T(4,128)(4,1)S(1)} %eq.98), kind=kOutput, calls=%fused_computation.33 | convolution fusion | flops 25329664 | bytes 340352 | tf_op jit(solution)/shard_map/dot_general | solution.py:43
  138.0 1.7 %all-to-all-done.3 = bf16[8,16,1024]{2,1,0:T(8,128)(2,1)S(1)} async-done(((bf16[8,16,1024]{2,1,0:T(8,128)(2,1)}), bf16[8,16,1024]{2,1,0:T(8,128)(2,1)S(1)}, u32[]{:S(2)}, u32[]{:S(2)}) %all-to-all-start.3) | async-done | bytes 262176 | tf_op jit(solution)/shard_map/all_to_all | solution.py:126
  139.7 0.8 convolution_reduce_fusion
  (7 shorter events, 0.0 us)
Async XLA Ops:
  7.2 25.2 %copy-start = (bf16[1,1024,768]{2,1,0:T(8,128)(2,1)S(1)}, bf16[1,1024,768]{2,1,0:T(8,128)(2,1)}, u32[]{:S(2)}) copy-start(bf16[1,1024,768]{2,1,0:T(8,128)(2,1)} %param.16) | copy-start | bytes 4718596
  7.2 13.3 %copy-start.5 = (f32[32,3]{0,1:T(4,128)S(1)}, f32[32,3]{0,1:T(4,128)}, u32[]{:S(2)}) copy-start(f32[32,3]{0,1:T(4,128)} %param.12) | copy-start | bytes 1156
  12.2 16.1 %all-to-all-start = ((bf16[8,16,1024]{2,1,0:T(8,128)(2,1)}), bf16[8,16,1024]{2,1,0:T(8,128)(2,1)S(1)}, u32[]{:S(2)}, u32[]{:S(2)}) async-start(bf16[8,16,1024]{2,1,0:T(8,128)(2,1)} %bitcast), calls=%async_computation | async-start | bytes 524288 | tf_op jit(solution)/shard_map/all_to_all | solution.py:78
  20.7 12.8 %copy-start.1 = (bf16[1,1024,768]{2,1,0:T(8,128)(2,1)S(1)}, bf16[1,1024,768]{2,1,0:T(8,128)(2,1)}, u32[]{:S(2)}) copy-start(bf16[1,1024,768]{2,1,0:T(8,128)(2,1)} %param.15) | copy-start | bytes 4718596
  28.3 13.8 %all-to-all-start.2 = ((bf16[8,16,1024]{2,1,0:T(8,128)(2,1)}), bf16[8,16,1024]{2,1,0:T(8,128)(2,1)}, u32[]{:S(2)}, u32[]{:S(2)}) async-start(bf16[8,16,1024]{2,1,0:T(8,128)(2,1)} %bitcast.73), calls=%async_computation.2 | async-start | bytes 524288 | tf_op jit(solution)/shard_map/all_to_all | solution.py:85
  32.4 58.1 %all-reduce.3.cloned.1.call-start = ((), (), s32[]{:S(2)}) async-start(), calls=%async_computation.4 | async-start | bytes 1179648 | tf_op jit(solution)/shard_map/psum | solution.py:102
  34.5 10.5 %copy-start.6 = (s32[8]{0:T(128)S(1)}, s32[8]{0:T(128)}, u32[]{:S(2)}) copy-start(s32[8]{0:T(128)} %param.13) | copy-start | bytes 100
  47.0 71.3 %collective-permute-start = (bf16[128,1024]{1,0:T(8,128)(2,1)S(1)}, bf16[128,1024]{1,0:T(8,128)(2,1)}, u32[]{:S(2)}, u32[]{:S(2)}) collective-permute-start(bf16[128,1024]{1,0:T(8,128)(2,1)S(1)} %bitcast.70), channel_id=1, source_target_pairs={{0,4},{1,5},{2,6},{3,7},{4,0},{5,1},{6,2},{7,3},{8,12},{9,13},{10,... | collective-permute-start | bytes 786440 | tf_op jit(solution)/shard_map/ppermute | solution.py:10
  47.1 83.0 %collective-permute-start.4 = (bf16[128,1024]{1,0:T(8,128)(2,1)}, bf16[128,1024]{1,0:T(8,128)(2,1)}, u32[]{:S(2)}, u32[]{:S(2)}) collective-permute-start(bf16[128,1024]{1,0:T(8,128)(2,1)} %bitcast.9), channel_id=1, source_target_pairs={{0,4},{1,5},{2,6},{3,7},{4,0},{5,1},{6,2},{7,3},{8,12},{9,13},{10,... | collective-permute-start | bytes 786440 | tf_op jit(solution)/shard_map/ppermute | solution.py:10
  95.2 23.1 %collective-permute-start.1 = (bf16[128,768]{1,0:T(8,128)(2,1)}, bf16[128,768]{1,0:T(8,128)(2,1)}, u32[]{:S(2)}, u32[]{:S(2)}) collective-permute-start(bf16[128,768]{1,0:T(8,128)(2,1)} %get-tuple-element.10), channel_id=1, source_target_pairs={{0,4},{1,5},{2,6},{3,7},{4,0},{5,1},{6,2},{7,3},{8,12},{9,13},{10,... | collective-permute-start | bytes 589832 | tf_op jit(solution)/shard_map/ppermute | solution.py:10
  100.0 3.3 %copy-start.2 = (bf16[1,768,1024]{2,1,0:T(8,128)(2,1)S(1)}, bf16[1,768,1024]{2,1,0:T(8,128)(2,1)}, u32[]{:S(2)}) copy-start(bf16[1,768,1024]{2,1,0:T(8,128)(2,1)} %param.17) | copy-start | bytes 4718596
  102.8 30.7 %collective-permute-start.2 = (bf16[128,768]{1,0:T(8,128)(2,1)}, bf16[128,768]{1,0:T(8,128)(2,1)}, u32[]{:S(2)}, u32[]{:S(2)}) collective-permute-start(bf16[128,768]{1,0:T(8,128)(2,1)} %get-tuple-element.11), channel_id=1, source_target_pairs={{0,4},{1,5},{2,6},{3,7},{4,0},{5,1},{6,2},{7,3},{8,12},{9,13},{10,... | collective-permute-start | bytes 589832 | tf_op jit(solution)/shard_map/ppermute | solution.py:10
  105.3 21.0 %all-to-all-start.1 = ((bf16[8,16,1024]{2,1,0:T(8,128)(2,1)}), bf16[8,16,1024]{2,1,0:T(8,128)(2,1)}, u32[]{:S(2)}, u32[]{:S(2)}) async-start(bf16[8,16,1024]{2,1,0:T(8,128)(2,1)} %bitcast.75), calls=%async_computation.1 | async-start | bytes 524288 | tf_op jit(solution)/shard_map/all_to_all | solution.py:119
  112.4 5.8 %copy-start.4 = (bf16[1024,768]{1,0:T(8,128)(2,1)S(1)}, bf16[1024,768]{1,0:T(8,128)(2,1)}, u32[]{:S(2)}) copy-start(bf16[1024,768]{1,0:T(8,128)(2,1)} %convolution_convert_fusion.5) | copy-start | bytes 4718596
  115.4 14.7 %collective-permute-start.3 = (bf16[128,768]{1,0:T(8,128)(2,1)}, bf16[128,768]{1,0:T(8,128)(2,1)}, u32[]{:S(2)}, u32[]{:S(2)}) collective-permute-start(bf16[128,768]{1,0:T(8,128)(2,1)} %get-tuple-element.12), channel_id=1, source_target_pairs={{0,4},{1,5},{2,6},{3,7},{4,0},{5,1},{6,2},{7,3},{8,12},{9,13},{10,... | collective-permute-start | bytes 589832 | tf_op jit(solution)/shard_map/ppermute | solution.py:10
  126.4 13.4 %all-to-all-start.3 = ((bf16[8,16,1024]{2,1,0:T(8,128)(2,1)}), bf16[8,16,1024]{2,1,0:T(8,128)(2,1)S(1)}, u32[]{:S(2)}, u32[]{:S(2)}) async-start(bf16[8,16,1024]{2,1,0:T(8,128)(2,1)} %bitcast.10), calls=%async_computation.3 | async-start | bytes 524288 | tf_op jit(solution)/shard_map/all_to_all | solution.py:126
  130.0 3.5 %copy-start.3 = (bf16[1024,768]{1,0:T(8,128)(2,1)S(1)}, bf16[1024,768]{1,0:T(8,128)(2,1)}, u32[]{:S(2)}) copy-start(bf16[1024,768]{1,0:T(8,128)(2,1)} %convolution_convert_fusion.3) | copy-start | bytes 4718596
Sparse Core Ops, SparseCore 0:
  45.1 45.3 all-reduce.2
where the time goes:
time: 148 us; the launch traced here: 147 us
  waiting for transfers between devices  60.5 us (41%)
  matrix products  35.7 us (24%)
  starting transfers between devices  27.5 us (19%)
  between operations  15.5 us (10%)
  other arithmetic  4.38 us (3%)
  local copies, waits for them, and re-layouts  3.78 us (3%)
    psum x1, waiting for transfers between devices, on_device(): lax.psum(up_part.astype(jnp.bfloat16), 'dp').astype(jnp.float32)  40.5 us
    dot_general x8, matrix products, row_contract(): lax.dot_general(left, right_mat, (((0,), (0,)), ((), ())), preferred_elem...  19.9 us
    ppermute x5, starting transfers between devices, shifted(): return lax.ppermute(value, axis, pairs)  8.82 us
    dot_general x3, matrix products, col_contract(): lax.dot_general(left, right_mat, (((1,), (1,)), ((), ())), preferred_elem...  7.69 us
    all_to_all x1, waiting for transfers between devices, on_device(): lax.all_to_all(send_back.reshape(slot_count, capacity, shard_width), 'exp...  7.53 us
    all_to_all x1, starting transfers between devices, on_device(): lax.all_to_all(send_rows.reshape(slot_count, capacity, shard_width), 'exp...  6.36 us
    all_to_all x1, waiting for transfers between devices, on_device(): lax.all_to_all(send_rows.reshape(slot_count, capacity, shard_width), 'exp...  5.49 us
    all_to_all x1, waiting for transfers between devices, on_device(): lax.all_to_all(slot_out.reshape(slot_count, capacity, shard_width), 'expe...  5.31 us
  transfers between devices with their start and end apart: 10, of which 5 were waited for; matrix products, arithmetic and copies ran while one was open for 24% of the time, Pallas kernels for 0%

commit v1 on v0

v1 whole, which is shorter than its diff:
```python
import jax
import jax.numpy as jnp
from jax import lax
from jax.sharding import PartitionSpec as P

CORES = 2


def peer(index, step, count):
    if count & (count - 1) == 0:
        return index ^ step
    return (index + step) % count


def place_of(block, index, count):
    if count & (count - 1) == 0:
        return block ^ index
    return (block - index) % count


def to_peer(value, step):
    count = lax.axis_size("dp")
    return lax.ppermute(value, "dp", [(i, peer(i, step, count)) for i in range(count)])


def from_peer(value, step):
    count = lax.axis_size("dp")
    return lax.ppermute(value, "dp", [(peer(i, step, count), i) for i in range(count)])


def to_chip(value, step):
    count = lax.axis_size("expert")
    pairs = [(i, (i + CORES * step) % count) for i in range(count)]
    return lax.ppermute(value, "expert", pairs)


def to_sibling(value):
    count = lax.axis_size("expert")
    return lax.ppermute(value, "expert", [(i, i ^ 1) for i in range(count)])


def swiglu(gate_pre, up_pre):
    return jax.nn.silu(gate_pre) * up_pre


def swiglu_back(gate_pre, up_pre, upstream):
    sigma = jax.nn.sigmoid(gate_pre)
    gate_back = upstream * up_pre * sigma * (1.0 + gate_pre * (1.0 - sigma))
    up_back = upstream * gate_pre * sigma
    return gate_back, up_back


def dot(left, right, left_dim, right_dim):
    return lax.dot_general(
        left, right, (((left_dim,), (right_dim,)), ((), ())), preferred_element_type=jnp.float32
    )


def split_weights(weights):
    high = lax.reduce_precision(weights, 8, 7)
    middle = lax.reduce_precision(weights - high, 8, 7)
    low = weights - high - middle
    return high, middle, low


def on_device(
    tokens, cotangent, expert_ids, gate_weights, slot_table, split_count, w_gate, w_up, w_down
):
    bf16, f32 = jnp.bfloat16, jnp.float32
    slot_count = slot_table.shape[0]
    expert_count = split_count.shape[0]
    token_count, top_k = expert_ids.shape
    width = tokens.shape[1]
    hidden = w_gate.shape[2]
    capacity = max(2, (token_count * top_k + expert_count - 1) // expert_count)
    dp = lax.axis_size("dp")
    chips = slot_count // CORES
    block = -(-slot_count * capacity // dp)
    rows = block * dp
    me = lax.axis_index("expert")
    mine = lax.axis_index("dp")

    high, middle, low = split_weights(gate_weights)
    meta = jnp.concatenate([expert_ids.astype(f32), high, middle, low], axis=1).astype(bf16)
    meta = jnp.pad(meta, ((0, 0), (0, -4 * top_k % 128)))
    packet = jnp.concatenate([tokens, cotangent, meta], axis=1)
    held = jnp.stack([packet] + [to_chip(packet, step) for step in range(1, chips)])
    got = jnp.stack([held, to_sibling(held)], axis=1)
    got = got.reshape(slot_count * token_count, packet.shape[1])
    chip, core = me // CORES, me % CORES
    step_iota = jnp.arange(chips, dtype=jnp.int32)
    chip_of = (chip - step_iota) % chips
    source = chip_of[:, None] * CORES + jnp.stack([core, 1 - core])[None, :]
    source = source.reshape(-1)

    meta_all = got[:, 2 * width :].astype(f32)
    ids = meta_all[:, :top_k].astype(jnp.int32)
    weight_parts = meta_all[:, top_k : 4 * top_k].reshape(-1, 3, top_k)
    weights = weight_parts[:, 0] + weight_parts[:, 1] + weight_parts[:, 2]
    slot_iota = jnp.arange(slot_count, dtype=jnp.int32)
    expert_iota = jnp.arange(expert_count, dtype=jnp.int32)

    def rows_of(slot):
        expert = jnp.sum(jnp.where(slot_iota == slot, slot_table, 0))
        same = slot_table == expert
        lower = jnp.min(jnp.where(same, slot_iota, slot_count))
        upper = jnp.max(jnp.where(same, slot_iota, -1))
        split = jnp.sum(jnp.where(expert_iota == expert, split_count, 0))
        taken = jnp.where(source < split, lower, upper) == slot
        named = ids == expert
        weight = jnp.sum(jnp.where(named, weights, 0.0), axis=1)
        chosen = jnp.any(named, axis=1).reshape(slot_count, token_count) & taken[:, None]
        counted = chosen.astype(jnp.int32)
        position = jnp.cumsum(counted, axis=1) - counted
        row = source[:, None] * capacity + position
        row = place_of(row // block, mine, dp) * block + row % block
        return jnp.where(chosen, row, -1).reshape(-1), weight, expert

    far_slot = (me + slot_count // 2) % slot_count
    own_row, own_weight, own_expert = rows_of(me)
    far_row, far_weight, far_expert = rows_of(far_slot)
    far_row = jnp.where(own_expert == far_expert, far_row, -1)
    row_iota = jnp.arange(rows, dtype=jnp.int32)[:, None]
    own_pick = row_iota == own_row[None, :]
    far_pick = row_iota == far_row[None, :]
    pick = jnp.concatenate([own_pick, far_pick], axis=0)
    token_weight = jnp.concatenate(
        [
            jnp.sum(jnp.where(own_pick, own_weight[None, :], 0.0), axis=1),
            jnp.sum(jnp.where(far_pick, far_weight[None, :], 0.0), axis=1),
        ]
    )
    pick = pick.astype(bf16)
    both_in = dot(pick, got[:, :width], 1, 0).astype(bf16)
    both_back = dot(pick, got[:, width : 2 * width], 1, 0)
    both_back = (token_weight[:, None] * both_back).astype(bf16)
    own_in, own_back = both_in[:rows], both_back[:rows]

    gate_mat, up_mat, down_mat = w_gate[0], w_up[0], w_down[0]
    partial = jnp.concatenate(
        [
            dot(own_in, gate_mat, 1, 0).astype(bf16),
            dot(own_in, up_mat, 1, 0).astype(bf16),
            dot(own_back, down_mat, 1, 1).astype(bf16),
        ],
        axis=1,
    ).reshape(dp, block, 3 * hidden)
    total = partial[0].astype(f32)
    for step in range(1, dp):
        total = total + to_peer(partial[step], step).astype(f32)
    gate_pre, up_pre, upstream = (total[:, i * hidden : (i + 1) * hidden] for i in range(3))
    gate_back, up_back = swiglu_back(gate_pre, up_pre, upstream)
    shard = jnp.concatenate(
        [
            swiglu(gate_pre, up_pre).astype(bf16),
            gate_back.astype(bf16),
            up_back.astype(bf16),
        ],
        axis=1,
    )
    far_shard = to_chip(shard, chips // 2)
    own_all = jnp.concatenate([shard] + [from_peer(shard, step) for step in range(1, dp)])
    far_all = jnp.concatenate([far_shard] + [from_peer(far_shard, step) for step in range(1, dp)])
    hidden_act = own_all[:, :hidden]
    gate_back = own_all[:, hidden : 2 * hidden]
    up_back = own_all[:, 2 * hidden :]

    slot_out = token_weight[:rows, None] * dot(hidden_act, down_mat, 1, 0)
    slot_dx = dot(gate_back, gate_mat, 1, 1) + dot(up_back, up_mat, 1, 1)
    result = jnp.concatenate([slot_out.astype(bf16), slot_dx.astype(bf16)], axis=1)
    spread = dot(pick[:rows], result, 0, 0).astype(bf16)
    spread = spread.reshape(chips, CORES, token_count, 2 * width)
    merged = spread[:, 0].astype(f32) + to_sibling(spread[:, 1]).astype(f32)
    home = merged[0]
    for step in range(1, chips):
        home = home + to_chip(merged[chips - step].astype(bf16), step).astype(f32)
    home = home.astype(bf16)

    both = jnp.concatenate([own_all, far_all], axis=0)
    gate_grad = dot(both_in, both[:, hidden : 2 * hidden], 0, 0).astype(bf16)
    up_grad = dot(both_in, both[:, 2 * hidden :], 0, 0).astype(bf16)
    down_grad = dot(both[:, :hidden], both_back, 0, 0).astype(bf16)
    return (home[:, :width], home[:, width:], gate_grad[None], up_grad[None], down_grad[None])


def solution(mesh):
    return jax.shard_map(
        on_device,
        mesh=mesh,
        in_specs=(
            P("expert", "dp"),
            P("expert", "dp"),
            P("expert", None),
            P("expert", None),
            P(),
            P(),
            P("expert", "dp", None),
            P("expert", "dp", None),
            P("expert", None, "dp"),
        ),
        out_specs=(
            P("expert", "dp"),
            P("expert", "dp"),
            P("expert", "dp", None),
            P("expert", "dp", None),
            P("expert", None, "dp"),
        ),
        check_vma=False,
    )
```

time: 148 us -> 92.1 us (0.62)
  waiting for transfers between devices: 60.5 us -> 32.1 us
  matrix products: 35.7 us -> 9.46 us
  between operations: 15.5 us -> 2.31 us
  other arithmetic: 4.38 us -> 15 us
    psum x1 -> x0, waiting for transfers between devices: 40.5 us -> none  [on_device(): lax.psum(up_part.astype(jnp.bfloat16), 'dp').astype(jnp.float32)]
    ppermute x5 -> x18, waiting for transfers between devices: 0.01 us -> 32.1 us  [the longest x7 16.8 us: to_chip(): return lax.ppermute(value, 'expert', pairs)]
    dot_general x16 -> x12, matrix products: 35.7 us -> 9.46 us  [dot(): lax.dot_general(left, right, (((left_dim,), (right_dim,)), ((), ())), pre...]
    all_to_all x4 -> x0, waiting for transfers between devices: 20 us -> none  [the longest x1 7.53 us: on_device(): lax.all_to_all(send_back.reshape(slot_count, capacity, shard_width), 'exp...]
    ppermute x5 -> x18, starting transfers between devices: 8.82 us -> 28.4 us  [the longest x7 17.6 us: to_chip(): return lax.ppermute(value, 'expert', pairs)]
    all_to_all x4 -> x0, starting transfers between devices: 18.7 us -> none  [the longest x1 6.36 us: on_device(): lax.all_to_all(send_rows.reshape(slot_count, capacity, shard_width), 'exp...]
    another operation x1 -> x9, other arithmetic: 0.14 us -> 4.25 us  [slot_choice(): before = jnp.cumsum(onehot, axis=0) - onehot]
    eq x1 -> x2, other arithmetic: 0.08 us -> 3.85 us  [the longest x1 3.81 us: rows_of(): taken = jnp.where(source < split, lower, upper) == slot]
  transfers between devices with their start and end apart: 10 -> 18, of which waited for: 5 -> 12; matrix products, arithmetic and copies ran while one was open for 24% -> 18% of each run, Pallas kernels for 0% -> 0%
where the time goes in v1:
time: 92.1 us; the launch traced here: 91.7 us
  waiting for transfers between devices  32.1 us (35%)
  starting transfers between devices  28.4 us (31%)
  other arithmetic  15 us (16%)
  matrix products  9.46 us (10%)
  local copies, waits for them, and re-layouts  4.42 us (5%)
  between operations  2.31 us (3%)
    ppermute x7, starting transfers between devices, to_chip(): return lax.ppermute(value, 'expert', pairs)  17.6 us
    ppermute x7, waiting for transfers between devices, to_chip(): return lax.ppermute(value, 'expert', pairs)  16.8 us
    dot_general x12, matrix products, dot(): lax.dot_general(left, right, (((left_dim,), (right_dim,)), ((), ())), pre...  9.46 us
    ppermute x3, waiting for transfers between devices, to_peer(): lax.ppermute(value, 'dp', [(i, peer(i, step, count)) for i in range(count)])  8.38 us
    ppermute x6, starting transfers between devices, from_peer(): lax.ppermute(value, 'dp', [(peer(i, step, count), i) for i in range(count)])  7.04 us
    ppermute x6, waiting for transfers between devices, from_peer(): lax.ppermute(value, 'dp', [(peer(i, step, count), i) for i in range(count)])  6.87 us
    eq x1, other arithmetic, rows_of(): taken = jnp.where(source < split, lower, upper) == slot  3.81 us
    ppermute x3, starting transfers between devices, to_peer(): lax.ppermute(value, 'dp', [(i, peer(i, step, count)) for i in range(count)])  3.55 us
  transfers between devices with their start and end apart: 18, of which 12 were waited for; matrix products, arithmetic and copies ran while one was open for 18% of the time, Pallas kernels for 0%

profile of v1, /device:TPU:0, one launch (start us, length us, event | category | flops | bytes accessed | tf_op | source)
XLA Modules:
  0.0 91.7 jit_solution(7060870876192468827)
XLA Ops:
  0.7 0.8 convert_convert_fusion
  1.5 0.7 reduce-precision_convert_fusion.1
  2.2 0.1 copy.53
  2.3 0.9 fusion.80
  3.2 4.1 %collective-permute-start.1 = (bf16[32,2176]{1,0:T(8,128)(2,1)S(1)}, bf16[32,2176]{1,0:T(8,128)(2,1)S(1)}, u32[]{:S(2)}, u32[]{:S(2)}) collective-permute-start(bf16[32,2176]{1,0:T(8,128)(2,1)S(1)} %get-tuple-element.35), channel_id=1, source_target_pairs={{0,4},{1,5},{2,6},{3,7},{4,0},{5,1},{6,2},{7,3},{8,12},{9,13},{10,... | collective-permute-start | bytes 417800 | tf_op jit(solution)/shard_map/ppermute | solution.py:34
  7.3 1.6 %collective-permute-start = (bf16[32,2176]{1,0:T(8,128)(2,1)S(1)}, bf16[32,2176]{1,0:T(8,128)(2,1)S(1)}, u32[]{:S(2)}, u32[]{:S(2)}) collective-permute-start(bf16[32,2176]{1,0:T(8,128)(2,1)S(1)} %get-tuple-element.35), channel_id=1, source_target_pairs={{0,2},{1,3},{2,4},{3,5},{4,6},{5,7},{6,0},{7,1},{8,10},{9,11},{10,... | collective-permute-start | bytes 417800 | tf_op jit(solution)/shard_map/ppermute | solution.py:34
  8.9 2.2 %collective-permute-start.2 = (bf16[32,2176]{1,0:T(8,128)(2,1)S(1)}, bf16[32,2176]{1,0:T(8,128)(2,1)S(1)}, u32[]{:S(2)}, u32[]{:S(2)}) collective-permute-start(bf16[32,2176]{1,0:T(8,128)(2,1)S(1)} %get-tuple-element.35), channel_id=1, source_target_pairs={{0,6},{1,7},{2,0},{3,1},{4,2},{5,3},{6,4},{7,5},{8,14},{9,15},{10,... | collective-permute-start | bytes 417800 | tf_op jit(solution)/shard_map/ppermute | solution.py:34
  11.4 6.5 %collective-permute-done.1 = bf16[32,2176]{1,0:T(8,128)(2,1)S(1)} collective-permute-done((bf16[32,2176]{1,0:T(8,128)(2,1)S(1)}, bf16[32,2176]{1,0:T(8,128)(2,1)S(1)}, u32[]{:S(2)}, u32[]{:S(2)}) %collective-permute-start.1) | collective-permute-done | bytes 139296 | tf_op jit(solution)/shard_map/ppermute | solution.py:34
  17.8 0.7 collective-permute-done.2
  18.5 0.1 fusion.82
  18.7 0.6 fusion.71
  20.7 2.0 %fusion.73 = (s32[]{:T(128)}, s32[]{:T(128)}) fusion(s32[6]{0:T(128)S(1)} %copy-done.4, s32[]{:T(128)} %get-tuple-element.13, s32[]{:T(128)} %get-tuple-element.14), kind=kLoop, calls=%fused_computation.137 | loop fusion | flops 34 | bytes 40 | tf_op jit(solution)/shard_map/reduce_sum | solution.py:108
  22.6 2.0 %fusion.67 = (s32[]{:T(128)}, s32[]{:T(128)}, s32[]{:T(128)}, s32[]{:T(128)}) fusion(s32[8]{0:T(128)S(1)} %copy-done.3, s32[]{:T(128)} %get-tuple-element.13, s32[]{:T(128)} %get-tuple-element.14), kind=kLoop, calls=%fused_computation.131 | loop fusion | flops 76 | bytes 56 | tf_op jit(solution)/shard_map/reduce_min | solution.py:106
  24.7 3.8 %select_compare_fusion.1 = (pred[4,2]{1,0:T(4,128)(4,1)S(1)}, pred[4,2]{1,0:T(4,128)(4,1)S(1)}) fusion(s32[]{:T(128)S(6)} %axis_index.22, s32[]{:T(128)} %get-tuple-element.10, s32[]{:T(128)} %get-tuple-element.9, s32[]{:T(128)} %get-tuple-element.7, s32[2]{0:T(128)S(1)} %pad_add_fusion.3, s32[4]{0:T(128)S(1)} %fusion.72, s32[]{:T(128)S(6)} %select_n.159, ...), kind=kLoop, calls=%fused_computation.104 | loop fusion | flops 56 | bytes 72 | tf_op jit(solution)/shard_map/eq | solution.py:109
  28.5 0.1 eq.122
  29.1 1.2 %pad_maximum_fusion = bf16[4,2,32,2176]{3,2,1,0:T(8,128)(2,1)S(1)} fusion(bf16[4,1,32,2176]{3,2,1,0:T(8,128)(2,1)} %bitcast.6, bf16[4,1,32,2176]{3,2,1,0:T(8,128)(2,1)S(1)} %get-tuple-element.24), kind=kLoop, calls=%fused_computation.29 | loop fusion | flops 557056 | bytes 2228224 | tf_op jit(solution)/shard_map/stack | solution.py:88
  30.3 1.4 %fusion.85 = (pred[256]{0:T(512)(128)(4,1)S(1)}, pred[256,3]{1,0:T(8,128)(4,1)S(1)}, pred[256]{0:T(512)(128)(4,1)S(1)}, pred[256,3]{1,0:T(8,128)(4,1)S(1)}) fusion(s32[]{:T(128)} %get-tuple-element.14, f32[256,128]{1,0:T(8,128)S(1)} %slice_convert_fusion.1, s32[]{:T(128)} %get-tuple-element.13), kind=kLoop, calls=%fused_computation.149 | loop fusion | flops 3328 | bytes 5128 | tf_op jit(solution)/shard_map/reduce_or | solution.py:112
  31.8 0.1 slice.134
  32.2 0.2 reduce_window_sum.21
  32.6 0.2 reduce_window_sum.23
  32.8 0.1 copy.49
  33.0 0.1 copy.48
  33.1 0.1 copy.50
  33.4 0.1 fusion.57
  33.5 0.1 select_reduce_fusion
  33.7 0.3 convolution_convert_fusion.4
  34.0 0.3 fusion.15
  34.3 0.8 copy-done.1
  35.1 0.4 fusion.31
  35.5 1.0 %copy-done.2 = bf16[1,1024,768]{2,1,0:T(8,128)(2,1)S(1)} copy-done((bf16[1,1024,768]{2,1,0:T(8,128)(2,1)S(1)}, bf16[1,1024,768]{2,1,0:T(8,128)(2,1)}, u32[]{:S(2)}) %copy-start.2) | copy-done | bytes 1572888
  36.5 0.4 fusion.28
  36.9 0.7 fusion.34
  37.6 1.6 %collective-permute-start.4 = (bf16[32,2304]{1,0:T(8,128)(2,1)S(1)}, bf16[32,2304]{1,0:T(8,128)(2,1)S(1)}, u32[]{:S(2)}, u32[]{:S(2)}) collective-permute-start(bf16[32,2304]{1,0:T(8,128)(2,1)S(1)} %get-tuple-element.21), channel_id=1, source_target_pairs={{0,8},{8,0},{16,24},{24,16},{1,9},{9,1},{17,25},{25,17},{2,10},{10... | collective-permute-start | bytes 442376 | tf_op jit(solution)/shard_map/ppermute | solution.py:23
  39.2 1.5 %collective-permute-start.6 = (bf16[32,2304]{1,0:T(8,128)(2,1)S(1)}, bf16[32,2304]{1,0:T(8,128)(2,1)S(1)}, u32[]{:S(2)}, u32[]{:S(2)}) collective-permute-start(bf16[32,2304]{1,0:T(8,128)(2,1)S(1)} %get-tuple-element.22), channel_id=1, source_target_pairs={{0,24},{8,16},{16,8},{24,0},{1,25},{9,17},{17,9},{25,1},{2,26},{10... | collective-permute-start | bytes 442376 | tf_op jit(solution)/shard_map/ppermute | solution.py:23
  40.7 0.5 collective-permute-start.5
  41.2 3.2 %collective-permute-done.4 = bf16[32,2304]{1,0:T(8,128)(2,1)S(1)} collective-permute-done((bf16[32,2304]{1,0:T(8,128)(2,1)S(1)}, bf16[32,2304]{1,0:T(8,128)(2,1)S(1)}, u32[]{:S(2)}, u32[]{:S(2)}) %collective-permute-start.4) | collective-permute-done | bytes 147488 | tf_op jit(solution)/shard_map/ppermute | solution.py:23
  44.4 3.8 %collective-permute-done.6 = bf16[32,2304]{1,0:T(8,128)(2,1)S(1)} collective-permute-done((bf16[32,2304]{1,0:T(8,128)(2,1)S(1)}, bf16[32,2304]{1,0:T(8,128)(2,1)S(1)}, u32[]{:S(2)}, u32[]{:S(2)}) %collective-permute-start.6) | collective-permute-done | bytes 147488 | tf_op jit(solution)/shard_map/ppermute | solution.py:23
  48.2 1.4 %collective-permute-done.5 = bf16[32,2304]{1,0:T(8,128)(2,1)S(1)} collective-permute-done((bf16[32,2304]{1,0:T(8,128)(2,1)S(1)}, bf16[32,2304]{1,0:T(8,128)(2,1)S(1)}, u32[]{:S(2)}, u32[]{:S(2)}) %collective-permute-start.5) | collective-permute-done | bytes 147488 | tf_op jit(solution)/shard_map/ppermute | solution.py:23
  49.7 1.5 %collective-permute-start.9 = (bf16[32,2304]{1,0:T(8,128)(2,1)S(1)}, bf16[32,2304]{1,0:T(8,128)(2,1)S(1)}, u32[]{:S(2)}, u32[]{:S(2)}) collective-permute-start(bf16[32,2304]{1,0:T(8,128)(2,1)S(1)} %get-tuple-element.33), channel_id=1, source_target_pairs={{24,0},{16,8},{8,16},{0,24},{25,1},{17,9},{9,17},{1,25},{26,2},{18... | collective-permute-start | bytes 442376 | tf_op jit(solution)/shard_map/ppermute | solution.py:28
  51.2 1.5 %collective-permute-start.8 = (bf16[32,2304]{1,0:T(8,128)(2,1)S(1)}, bf16[32,2304]{1,0:T(8,128)(2,1)S(1)}, u32[]{:S(2)}, u32[]{:S(2)}) collective-permute-start(bf16[32,2304]{1,0:T(8,128)(2,1)S(1)} %get-tuple-element.33), channel_id=1, source_target_pairs={{16,0},{24,8},{0,16},{8,24},{17,1},{25,9},{1,17},{9,25},{18,2},{26... | collective-permute-start | bytes 442376 | tf_op jit(solution)/shard_map/ppermute | solution.py:28
  52.7 0.5 collective-permute-start.7
  53.3 4.0 %collective-permute-start.14 = (bf16[32,2304]{1,0:T(8,128)(2,1)S(1)}, bf16[32,2304]{1,0:T(8,128)(2,1)S(1)}, u32[]{:S(2)}, u32[]{:S(2)}) collective-permute-start(bf16[32,2304]{1,0:T(8,128)(2,1)S(1)} %get-tuple-element.33), channel_id=1, source_target_pairs={{0,4},{1,5},{2,6},{3,7},{4,0},{5,1},{6,2},{7,3},{8,12},{9,13},{10,... | collective-permute-start | bytes 442376 | tf_op jit(solution)/shard_map/ppermute | solution.py:34
  57.3 1.4 %collective-permute-done.8 = bf16[32,2304]{1,0:T(8,128)(2,1)S(1)} collective-permute-done((bf16[32,2304]{1,0:T(8,128)(2,1)S(1)}, bf16[32,2304]{1,0:T(8,128)(2,1)S(1)}, u32[]{:S(2)}, u32[]{:S(2)}) %collective-permute-start.8) | collective-permute-done | bytes 147488 | tf_op jit(solution)/shard_map/ppermute | solution.py:28
  58.7 0.4 fusion.22
  59.1 0.6 fusion.4
  59.7 0.6 fusion.25
  60.4 0.5 convolution_convert_fusion
  61.0 1.6 %collective-permute-done.14 = bf16[32,2304]{1,0:T(8,128)(2,1)S(1)} collective-permute-done((bf16[32,2304]{1,0:T(8,128)(2,1)S(1)}, bf16[32,2304]{1,0:T(8,128)(2,1)S(1)}, u32[]{:S(2)}, u32[]{:S(2)}) %collective-permute-start.14) | collective-permute-done | bytes 147488 | tf_op jit(solution)/shard_map/ppermute | solution.py:34
  62.7 1.4 %collective-permute-start.17 = (bf16[32,2304]{1,0:T(8,128)(2,1)S(1)}, bf16[32,2304]{1,0:T(8,128)(2,1)S(1)}, u32[]{:S(2)}, u32[]{:S(2)}) collective-permute-start(bf16[32,2304]{1,0:T(8,128)(2,1)S(1)} %collective-permute-done.14), channel_id=1, source_target_pairs={{24,0},{16,8},{8,16},{0,24},{25,1},{17,9},{9,17},{1,25},{26,2},{18... | collective-permute-start | bytes 442376 | tf_op jit(solution)/shard_map/ppermute | solution.py:28
  64.1 1.5 %collective-permute-start.16 = (bf16[32,2304]{1,0:T(8,128)(2,1)S(1)}, bf16[32,2304]{1,0:T(8,128)(2,1)S(1)}, u32[]{:S(2)}, u32[]{:S(2)}) collective-permute-start(bf16[32,2304]{1,0:T(8,128)(2,1)S(1)} %collective-permute-done.14), channel_id=1, source_target_pairs={{16,0},{24,8},{0,16},{8,24},{17,1},{25,9},{1,17},{9,25},{18,2},{26... | collective-permute-start | bytes 442376 | tf_op jit(solution)/shard_map/ppermute | solution.py:28
  65.6 0.5 collective-permute-start.15
  66.2 4.7 %collective-permute-done.15 = bf16[32,2304]{1,0:T(8,128)(2,1)S(1)} collective-permute-done((bf16[32,2304]{1,0:T(8,128)(2,1)S(1)}, bf16[32,2304]{1,0:T(8,128)(2,1)S(1)}, u32[]{:S(2)}, u32[]{:S(2)}) %collective-permute-start.15) | collective-permute-done | bytes 147488 | tf_op jit(solution)/shard_map/ppermute | solution.py:28
  70.9 0.8 collective-permute-done.16
  71.7 1.8 %fusion.13 = bf16[1,1024,768]{2,1,0:T(8,128)(2,1)} fusion(bf16[256,1024]{1,0:T(8,128)(2,1)S(1)} %convolution_convert_fusion.4, bf16[256,2304]{1,0:T(8,128)(2,1)S(1)} %constant_dynamic-update-slice_fusion), kind=kOutput, calls=%fused_computation.17 | convolution fusion | flops 403439616 | bytes 2490368 | tf_op jit(solution)/shard_map/dot_general | solution.py:54
  73.5 1.8 %fusion.12 = bf16[1,1024,768]{2,1,0:T(8,128)(2,1)} fusion(bf16[256,1024]{1,0:T(8,128)(2,1)S(1)} %convolution_convert_fusion.4, bf16[256,2304]{1,0:T(8,128)(2,1)S(1)} %constant_dynamic-update-slice_fusion), kind=kOutput, calls=%fused_computation.16 | convolution fusion | flops 403439616 | bytes 2490368 | tf_op jit(solution)/shard_map/dot_general | solution.py:54
  75.3 0.1 fusion.81
  75.5 1.8 %collective-permute-start.11 = (bf16[32,2048]{1,0:T(8,128)(2,1)S(1)}, bf16[32,2048]{1,0:T(8,128)(2,1)S(1)}, u32[]{:S(2)}, u32[]{:S(2)}) collective-permute-start(bf16[32,2048]{1,0:T(8,128)(2,1)S(1)} %get-tuple-element.26), channel_id=1, source_target_pairs={{0,2},{1,3},{2,4},{3,5},{4,6},{5,7},{6,0},{7,1},{8,10},{9,11},{10,... | collective-permute-start | bytes 393224 | tf_op jit(solution)/shard_map/ppermute | solution.py:34
  77.2 2.1 %collective-permute-start.13 = (bf16[32,2048]{1,0:T(8,128)(2,1)S(1)}, bf16[32,2048]{1,0:T(8,128)(2,1)S(1)}, u32[]{:S(2)}, u32[]{:S(2)}) collective-permute-start(bf16[32,2048]{1,0:T(8,128)(2,1)S(1)} %get-tuple-element.27), channel_id=1, source_target_pairs={{0,6},{1,7},{2,0},{3,1},{4,2},{5,3},{6,4},{7,5},{8,14},{9,15},{10,... | collective-permute-start | bytes 393224 | tf_op jit(solution)/shard_map/ppermute | solution.py:34
  79.3 1.8 %collective-permute-start.12 = (bf16[32,2048]{1,0:T(8,128)(2,1)S(1)}, bf16[32,2048]{1,0:T(8,128)(2,1)S(1)}, u32[]{:S(2)}, u32[]{:S(2)}) collective-permute-start(bf16[32,2048]{1,0:T(8,128)(2,1)S(1)} %get-tuple-element.28), channel_id=1, source_target_pairs={{0,4},{1,5},{2,6},{3,7},{4,0},{5,1},{6,2},{7,3},{8,12},{9,13},{10,... | collective-permute-start | bytes 393224 | tf_op jit(solution)/shard_map/ppermute | solution.py:34
  81.2 1.7 %fusion.14 = bf16[1,768,1024]{2,1,0:T(8,128)(2,1)} fusion(bf16[256,1024]{1,0:T(8,128)(2,1)S(1)} %fusion.15, bf16[256,2304]{1,0:T(8,128)(2,1)S(1)} %constant_dynamic-update-slice_fusion), kind=kOutput, calls=%fused_computation.18 | convolution fusion | flops 403439616 | bytes 2490368 | tf_op jit(solution)/shard_map/dot_general | solution.py:54
  82.9 0.6 collective-permute-done.11
  83.5 1.7 %collective-permute-done.13 = bf16[32,2048]{1,0:T(8,128)(2,1)S(1)} collective-permute-done((bf16[32,2048]{1,0:T(8,128)(2,1)S(1)}, bf16[32,2048]{1,0:T(8,128)(2,1)S(1)}, u32[]{:S(2)}, u32[]{:S(2)}) %collective-permute-start.13) | collective-permute-done | bytes 131104 | tf_op jit(solution)/shard_map/ppermute | solution.py:34
  85.2 5.7 %collective-permute-done.12 = bf16[32,2048]{1,0:T(8,128)(2,1)S(1)} collective-permute-done((bf16[32,2048]{1,0:T(8,128)(2,1)S(1)}, bf16[32,2048]{1,0:T(8,128)(2,1)S(1)}, u32[]{:S(2)}, u32[]{:S(2)}) %collective-permute-start.12) | collective-permute-done | bytes 131104 | tf_op jit(solution)/shard_map/ppermute | solution.py:34
  91.0 0.7 fusion.88
  (57 shorter events, 2.1 us)
Async XLA Ops:
  0.6 36.2 %copy-start = (bf16[1,768,1024]{2,1,0:T(8,128)(2,1)S(1)}, bf16[1,768,1024]{2,1,0:T(8,128)(2,1)}, u32[]{:S(2)}) copy-start(bf16[1,768,1024]{2,1,0:T(8,128)(2,1)} %param.17) | copy-start | bytes 4718596
  0.6 18.1 %copy-start.3 = (s32[8]{0:T(128)S(1)}, s32[8]{0:T(128)}, u32[]{:S(2)}) copy-start(s32[8]{0:T(128)} %param.13) | copy-start | bytes 100
  0.7 20.0 %copy-start.4 = (s32[6]{0:T(128)S(1)}, s32[6]{0:T(128)}, u32[]{:S(2)}) copy-start(s32[6]{0:T(128)} %param.14) | copy-start | bytes 76
  3.2 14.7 %collective-permute-start.1 = (bf16[32,2176]{1,0:T(8,128)(2,1)S(1)}, bf16[32,2176]{1,0:T(8,128)(2,1)S(1)}, u32[]{:S(2)}, u32[]{:S(2)}) collective-permute-start(bf16[32,2176]{1,0:T(8,128)(2,1)S(1)} %get-tuple-element.35), channel_id=1, source_target_pairs={{0,4},{1,5},{2,6},{3,7},{4,0},{5,1},{6,2},{7,3},{8,12},{9,13},{10,... | collective-permute-start | bytes 417800 | tf_op jit(solution)/shard_map/ppermute | solution.py:34
  7.3 10.5 %collective-permute-start = (bf16[32,2176]{1,0:T(8,128)(2,1)S(1)}, bf16[32,2176]{1,0:T(8,128)(2,1)S(1)}, u32[]{:S(2)}, u32[]{:S(2)}) collective-permute-start(bf16[32,2176]{1,0:T(8,128)(2,1)S(1)} %get-tuple-element.35), channel_id=1, source_target_pairs={{0,2},{1,3},{2,4},{3,5},{4,6},{5,7},{6,0},{7,1},{8,10},{9,11},{10,... | collective-permute-start | bytes 417800 | tf_op jit(solution)/shard_map/ppermute | solution.py:34
  8.9 9.7 %collective-permute-start.2 = (bf16[32,2176]{1,0:T(8,128)(2,1)S(1)}, bf16[32,2176]{1,0:T(8,128)(2,1)S(1)}, u32[]{:S(2)}, u32[]{:S(2)}) collective-permute-start(bf16[32,2176]{1,0:T(8,128)(2,1)S(1)} %get-tuple-element.35), channel_id=1, source_target_pairs={{0,6},{1,7},{2,0},{3,1},{4,2},{5,3},{6,4},{7,5},{8,14},{9,15},{10,... | collective-permute-start | bytes 417800 | tf_op jit(solution)/shard_map/ppermute | solution.py:34
  18.6 10.5 %collective-permute-start.3 = (bf16[4,32,2176]{2,1,0:T(8,128)(2,1)S(1)}, bf16[4,32,2176]{2,1,0:T(8,128)(2,1)}, u32[]{:S(2)}, u32[]{:S(2)}) collective-permute-start(bf16[4,32,2176]{2,1,0:T(8,128)(2,1)S(1)} %get-tuple-element.25), channel_id=1, source_target_pairs={{0,1},{1,0},{2,3},{3,2},{4,5},{5,4},{6,7},{7,6},{8,9},{9,8},{10,11... | collective-permute-start | bytes 1671176 | tf_op jit(solution)/shard_map/ppermute | solution.py:39
  33.6 1.4 %copy-start.1 = (bf16[1,1024,768]{2,1,0:T(8,128)(2,1)S(1)}, bf16[1,1024,768]{2,1,0:T(8,128)(2,1)}, u32[]{:S(2)}) copy-start(bf16[1,1024,768]{2,1,0:T(8,128)(2,1)} %param.16) | copy-start | bytes 4718596
  35.1 1.4 %copy-start.2 = (bf16[1,1024,768]{2,1,0:T(8,128)(2,1)S(1)}, bf16[1,1024,768]{2,1,0:T(8,128)(2,1)}, u32[]{:S(2)}) copy-start(bf16[1,1024,768]{2,1,0:T(8,128)(2,1)} %param.15) | copy-start | bytes 4718596
  37.6 6.8 %collective-permute-start.4 = (bf16[32,2304]{1,0:T(8,128)(2,1)S(1)}, bf16[32,2304]{1,0:T(8,128)(2,1)S(1)}, u32[]{:S(2)}, u32[]{:S(2)}) collective-permute-start(bf16[32,2304]{1,0:T(8,128)(2,1)S(1)} %get-tuple-element.21), channel_id=1, source_target_pairs={{0,8},{8,0},{16,24},{24,16},{1,9},{9,1},{17,25},{25,17},{2,10},{10... | collective-permute-start | bytes 442376 | tf_op jit(solution)/shard_map/ppermute | solution.py:23
  39.2 9.0 %collective-permute-start.6 = (bf16[32,2304]{1,0:T(8,128)(2,1)S(1)}, bf16[32,2304]{1,0:T(8,128)(2,1)S(1)}, u32[]{:S(2)}, u32[]{:S(2)}) collective-permute-start(bf16[32,2304]{1,0:T(8,128)(2,1)S(1)} %get-tuple-element.22), channel_id=1, source_target_pairs={{0,24},{8,16},{16,8},{24,0},{1,25},{9,17},{17,9},{25,1},{2,26},{10... | collective-permute-start | bytes 442376 | tf_op jit(solution)/shard_map/ppermute | solution.py:23
  40.7 8.8 %collective-permute-start.5 = (bf16[32,2304]{1,0:T(8,128)(2,1)S(1)}, bf16[32,2304]{1,0:T(8,128)(2,1)S(1)}, u32[]{:S(2)}, u32[]{:S(2)}) collective-permute-start(bf16[32,2304]{1,0:T(8,128)(2,1)S(1)} %get-tuple-element.23), channel_id=1, source_target_pairs={{0,16},{8,24},{16,0},{24,8},{1,17},{9,25},{17,1},{25,9},{2,18},{10... | collective-permute-start | bytes 442376 | tf_op jit(solution)/shard_map/ppermute | solution.py:23
  49.7 7.5 %collective-permute-start.9 = (bf16[32,2304]{1,0:T(8,128)(2,1)S(1)}, bf16[32,2304]{1,0:T(8,128)(2,1)S(1)}, u32[]{:S(2)}, u32[]{:S(2)}) collective-permute-start(bf16[32,2304]{1,0:T(8,128)(2,1)S(1)} %get-tuple-element.33), channel_id=1, source_target_pairs={{24,0},{16,8},{8,16},{0,24},{25,1},{17,9},{9,17},{1,25},{26,2},{18... | collective-permute-start | bytes 442376 | tf_op jit(solution)/shard_map/ppermute | solution.py:28
  51.2 7.4 %collective-permute-start.8 = (bf16[32,2304]{1,0:T(8,128)(2,1)S(1)}, bf16[32,2304]{1,0:T(8,128)(2,1)S(1)}, u32[]{:S(2)}, u32[]{:S(2)}) collective-permute-start(bf16[32,2304]{1,0:T(8,128)(2,1)S(1)} %get-tuple-element.33), channel_id=1, source_target_pairs={{16,0},{24,8},{0,16},{8,24},{17,1},{25,9},{1,17},{9,25},{18,2},{26... | collective-permute-start | bytes 442376 | tf_op jit(solution)/shard_map/ppermute | solution.py:28
  52.7 5.9 %collective-permute-start.7 = (bf16[32,2304]{1,0:T(8,128)(2,1)S(1)}, bf16[32,2304]{1,0:T(8,128)(2,1)S(1)}, u32[]{:S(2)}, u32[]{:S(2)}) collective-permute-start(bf16[32,2304]{1,0:T(8,128)(2,1)S(1)} %get-tuple-element.33), channel_id=1, source_target_pairs={{8,0},{0,8},{24,16},{16,24},{9,1},{1,9},{25,17},{17,25},{10,2},{2,... | collective-permute-start | bytes 442376 | tf_op jit(solution)/shard_map/ppermute | solution.py:28
  53.3 9.4 %collective-permute-start.14 = (bf16[32,2304]{1,0:T(8,128)(2,1)S(1)}, bf16[32,2304]{1,0:T(8,128)(2,1)S(1)}, u32[]{:S(2)}, u32[]{:S(2)}) collective-permute-start(bf16[32,2304]{1,0:T(8,128)(2,1)S(1)} %get-tuple-element.33), channel_id=1, source_target_pairs={{0,4},{1,5},{2,6},{3,7},{4,0},{5,1},{6,2},{7,3},{8,12},{9,13},{10,... | collective-permute-start | bytes 442376 | tf_op jit(solution)/shard_map/ppermute | solution.py:34
  60.9 14.3 %collective-permute-start.10 = (bf16[4,32,2048]{2,1,0:T(8,128)(2,1)S(1)}, bf16[4,32,2048]{2,1,0:T(8,128)(2,1)S(1)}, u32[]{:S(2)}, u32[]{:S(2)}) collective-permute-start(bf16[4,32,2048]{2,1,0:T(8,128)(2,1)S(1)} %slice_bitcast_fusion), channel_id=1, source_target_pairs={{0,1},{1,0},{2,3},{3,2},{4,5},{5,4},{6,7},{7,6},{8,9},{9,8},{10,11... | collective-permute-start | bytes 1572872 | tf_op jit(solution)/shard_map/ppermute | solution.py:39
  62.7 9.1 %collective-permute-start.17 = (bf16[32,2304]{1,0:T(8,128)(2,1)S(1)}, bf16[32,2304]{1,0:T(8,128)(2,1)S(1)}, u32[]{:S(2)}, u32[]{:S(2)}) collective-permute-start(bf16[32,2304]{1,0:T(8,128)(2,1)S(1)} %collective-permute-done.14), channel_id=1, source_target_pairs={{24,0},{16,8},{8,16},{0,24},{25,1},{17,9},{9,17},{1,25},{26,2},{18... | collective-permute-start | bytes 442376 | tf_op jit(solution)/shard_map/ppermute | solution.py:28
  64.1 7.6 %collective-permute-start.16 = (bf16[32,2304]{1,0:T(8,128)(2,1)S(1)}, bf16[32,2304]{1,0:T(8,128)(2,1)S(1)}, u32[]{:S(2)}, u32[]{:S(2)}) collective-permute-start(bf16[32,2304]{1,0:T(8,128)(2,1)S(1)} %collective-permute-done.14), channel_id=1, source_target_pairs={{16,0},{24,8},{0,16},{8,24},{17,1},{25,9},{1,17},{9,25},{18,2},{26... | collective-permute-start | bytes 442376 | tf_op jit(solution)/shard_map/ppermute | solution.py:28
  65.6 5.3 %collective-permute-start.15 = (bf16[32,2304]{1,0:T(8,128)(2,1)S(1)}, bf16[32,2304]{1,0:T(8,128)(2,1)S(1)}, u32[]{:S(2)}, u32[]{:S(2)}) collective-permute-start(bf16[32,2304]{1,0:T(8,128)(2,1)S(1)} %collective-permute-done.14), channel_id=1, source_target_pairs={{8,0},{0,8},{24,16},{16,24},{9,1},{1,9},{25,17},{17,25},{10,2},{2,... | collective-permute-start | bytes 442376 | tf_op jit(solution)/shard_map/ppermute | solution.py:28
  75.5 8.1 %collective-permute-start.11 = (bf16[32,2048]{1,0:T(8,128)(2,1)S(1)}, bf16[32,2048]{1,0:T(8,128)(2,1)S(1)}, u32[]{:S(2)}, u32[]{:S(2)}) collective-permute-start(bf16[32,2048]{1,0:T(8,128)(2,1)S(1)} %get-tuple-element.26), channel_id=1, source_target_pairs={{0,2},{1,3},{2,4},{3,5},{4,6},{5,7},{6,0},{7,1},{8,10},{9,11},{10,... | collective-permute-start | bytes 393224 | tf_op jit(solution)/shard_map/ppermute | solution.py:34
  77.2 8.0 %collective-permute-start.13 = (bf16[32,2048]{1,0:T(8,128)(2,1)S(1)}, bf16[32,2048]{1,0:T(8,128)(2,1)S(1)}, u32[]{:S(2)}, u32[]{:S(2)}) collective-permute-start(bf16[32,2048]{1,0:T(8,128)(2,1)S(1)} %get-tuple-element.27), channel_id=1, source_target_pairs={{0,6},{1,7},{2,0},{3,1},{4,2},{5,3},{6,4},{7,5},{8,14},{9,15},{10,... | collective-permute-start | bytes 393224 | tf_op jit(solution)/shard_map/ppermute | solution.py:34
  79.3 11.6 %collective-permute-start.12 = (bf16[32,2048]{1,0:T(8,128)(2,1)S(1)}, bf16[32,2048]{1,0:T(8,128)(2,1)S(1)}, u32[]{:S(2)}, u32[]{:S(2)}) collective-permute-start(bf16[32,2048]{1,0:T(8,128)(2,1)S(1)} %get-tuple-element.28), channel_id=1, source_target_pairs={{0,4},{1,5},{2,6},{3,7},{4,0},{5,1},{6,2},{7,3},{8,12},{9,13},{10,... | collective-permute-start | bytes 393224 | tf_op jit(solution)/shard_map/ppermute | solution.py:34

commit v2 on v1

v2 whole, which is shorter than its diff:
```python
import functools

import jax
import jax.numpy as jnp
from jax import lax
from jax.experimental import pallas as pl
from jax.experimental.pallas import tpu as pltpu
from jax.sharding import PartitionSpec as P


CORES = 2
LANES = 128


def peer(index, step, count):
    if count & (count - 1) == 0:
        return index ^ step
    return (index + step) % count


def to_peer(value, step):
    count = lax.axis_size("dp")
    return lax.ppermute(value, "dp", [(i, peer(i, step, count)) for i in range(count)])


def from_peer(value, step):
    count = lax.axis_size("dp")
    return lax.ppermute(value, "dp", [(peer(i, step, count), i) for i in range(count)])


def to_chip(value, step):
    count = lax.axis_size("expert")
    pairs = [(i, (i + CORES * step) % count) for i in range(count)]
    return lax.ppermute(value, "expert", pairs)


def to_sibling(value):
    count = lax.axis_size("expert")
    return lax.ppermute(value, "expert", [(i, i ^ 1) for i in range(count)])


def dot(left, right, left_dim, right_dim):
    return lax.dot_general(
        left, right, (((left_dim,), (right_dim,)), ((), ())), preferred_element_type=jnp.float32
    )


def whole_part(value, divisor):
    return jnp.floor((value.astype(jnp.float32) + 0.5) * (1.0 / divisor)).astype(jnp.int32)


def grant(mesh_small):
    return pltpu.CompilerParams(vmem_limit_bytes=(10 if mesh_small else 48) << 20)


def pack_kernel(token_ref, id_ref, weight_ref, out_ref):
    bf16, f32 = jnp.bfloat16, jnp.float32
    width = token_ref.shape[1]
    rows, extra = out_ref.shape[0], out_ref.shape[1] - width
    out_ref[:, :width] = token_ref[...]
    weights = weight_ref[...]
    high = weights.astype(bf16).astype(f32)
    middle = (weights - high).astype(bf16).astype(f32)
    pieces = [id_ref[...].astype(f32), high, middle, weights - high - middle]
    pieces.append(jnp.zeros((extra - 4 * weights.shape[0], rows), f32))
    out_ref[:, width:] = jnp.concatenate(pieces, axis=0).T.astype(bf16)


def pack(tokens, expert_ids, gate_weights):
    rows, width = tokens.shape
    top_k = expert_ids.shape[1]
    extra = -(-4 * top_k // LANES) * LANES
    vmem = pl.BlockSpec(memory_space=pltpu.VMEM)
    return pl.pallas_call(
        pack_kernel,
        out_shape=jax.ShapeDtypeStruct((rows, width + extra), jnp.bfloat16),
        in_specs=[vmem] * 3,
        out_specs=vmem,
        compiler_params=grant(True),
    )(tokens, expert_ids.T, gate_weights.T)


def joined(refs):
    return jnp.concatenate([ref[...] for ref in refs], axis=0)


def route_kernel(sizes, table_ref, split_ref, *refs):
    token_count, top_k, width, capacity, block, dp, chips = sizes
    data_refs, (pick_ref, scale_ref, all_ref, own_ref) = refs[:-4], refs[-4:]
    bf16, f32 = jnp.bfloat16, jnp.float32
    slot_count = chips * CORES
    half = chips * token_count
    rows = block * dp
    me = lax.axis_index("expert")
    mine = lax.axis_index("dp")
    partner = lax.rem(me + slot_count // 2, slot_count)
    expert = table_ref[me]
    paired = (expert == table_ref[partner]).astype(jnp.int32)
    split = split_ref[expert]
    lower = (me < slot_count // 2).astype(jnp.int32)
    chip, core = me // CORES, lax.rem(me, CORES)

    count = CORES * half
    data = joined(data_refs)
    meta = data[:, width:].astype(f32)
    named = jnp.zeros((count, 1), jnp.bool_)
    pieces = [jnp.zeros((count, 1), f32) for _ in range(3)]
    for k in range(top_k):
        hit = meta[:, k : k + 1] == expert.astype(f32)
        named = named | hit
        for i in range(3):
            first = top_k * (i + 1) + k
            pieces[i] = pieces[i] + jnp.where(hit, meta[:, first : first + 1], 0.0)
    token = lax.broadcasted_iota(jnp.int32, (count, 1), 0)
    part = (token >= half).astype(jnp.int32)
    chip_of = chip - whole_part(token - part * half, token_count)
    chip_of = jnp.where(chip_of < 0, chip_of + chips, chip_of)
    source = chip_of * CORES + jnp.where(part == 0, core, 1 - core)
    in_lower = (source < split).astype(jnp.int32)
    taken = (paired == 0) | (in_lower == lower)
    at = lax.broadcasted_iota(jnp.int32, (half, half), 0)
    before = lax.broadcasted_iota(jnp.int32, (half, half), 1)
    same = whole_part(at, token_count) == whole_part(before, token_count)
    earlier = jnp.where(same & (before < at), 1.0, 0.0).astype(bf16)
    counted = jnp.broadcast_to(jnp.where(named, 1.0, 0.0), (count, LANES)).astype(bf16)
    position = jnp.concatenate(
        [dot(earlier, counted[:half], 1, 0), dot(earlier, counted[half:], 1, 0)], axis=0
    )[:, :1].astype(jnp.int32)
    row = source * capacity + position
    row_block = whole_part(row, block)
    if dp & (dp - 1) == 0:
        place = row_block ^ mine
    else:
        place = row_block - mine
        place = jnp.where(place < 0, place + dp, place)
    row = jnp.where(named, (place - row_block) * block + row, -1)
    row_lane = lax.broadcasted_iota(jnp.int32, (count, rows), 1)
    pick = jnp.where(row_lane == row, 1.0, 0.0).T.astype(bf16)
    pick_ref[...] = pick
    lane = lax.broadcasted_iota(jnp.int32, (count, LANES), 1)
    facts = jnp.where(lane == 3, jnp.where(taken, 1.0, 0.0), 0.0)
    for i in range(3):
        facts = jnp.where(lane == i, pieces[i], facts)
    scale = dot(pick, facts.astype(bf16), 1, 0)
    gathered = dot(pick, data[:, :width], 1, 0)
    own = scale[:, 3:4]
    weight = scale[:, 0:1] + scale[:, 1:2] + scale[:, 2:3]
    column = lax.broadcasted_iota(jnp.int32, (rows, LANES), 1)
    scale_ref[...] = jnp.where(
        column == 0, weight, jnp.where(column == 1, weight * own, paired.astype(f32))
    )
    all_ref[...] = gathered.astype(bf16)
    own_ref[...] = (gathered * own).astype(bf16)


def route(slot_table, split_count, packets, sizes):
    token_count, _, width, _, block, dp, chips = sizes
    rows, half = block * dp, chips * token_count
    smem = pl.BlockSpec(memory_space=pltpu.SMEM)
    vmem = pl.BlockSpec(memory_space=pltpu.VMEM)
    return pl.pallas_call(
        functools.partial(route_kernel, sizes),
        out_shape=(
            jax.ShapeDtypeStruct((rows, CORES * half), jnp.bfloat16),
            jax.ShapeDtypeStruct((rows, LANES), jnp.float32),
            jax.ShapeDtypeStruct((rows, width), jnp.bfloat16),
            jax.ShapeDtypeStruct((rows, width), jnp.bfloat16),
        ),
        in_specs=[smem, smem] + [vmem] * len(packets),
        out_specs=(vmem, vmem, vmem, vmem),
        compiler_params=grant(chips <= 4),
        cost_estimate=pl.CostEstimate(
            flops=4 * rows * half * width, bytes_accessed=8 * half * width, transcendentals=0
        ),
    )(slot_table, split_count, *packets)


def back_kernel(pick_ref, scale_ref, *refs):
    data_refs, (all_ref, own_ref) = refs[:-2], refs[-2:]
    back = dot(pick_ref[...], joined(data_refs), 1, 0)
    all_ref[...] = (scale_ref[:, 0:1] * back).astype(jnp.bfloat16)
    own_ref[...] = (scale_ref[:, 1:2] * back).astype(jnp.bfloat16)


def backward_rows(pick, scale, cots):
    rows, width = pick.shape[0], cots[0].shape[-1]
    vmem = pl.BlockSpec(memory_space=pltpu.VMEM)
    shape = jax.ShapeDtypeStruct((rows, width), jnp.bfloat16)
    return pl.pallas_call(
        back_kernel,
        out_shape=(shape, shape),
        in_specs=[vmem] * (2 + len(cots)),
        out_specs=(vmem, vmem),
        compiler_params=grant(len(cots) > 2),
        cost_estimate=pl.CostEstimate(
            flops=2 * rows * pick.shape[1] * width,
            bytes_accessed=2 * pick.shape[1] * width,
            transcendentals=0,
        ),
    )(pick, scale, *cots)


def gathered(value, chips):
    blocks = [value]
    for step in range(1, chips):
        blocks.append(to_chip(value, step))
    if chips > 4:
        blocks = [jnp.concatenate(blocks)]
    others = []
    for item in blocks:
        others.append(to_sibling(item))
    return blocks + others


def on_device(
    tokens, cotangent, expert_ids, gate_weights, slot_table, split_count, w_gate, w_up, w_down
):
    bf16, f32 = jnp.bfloat16, jnp.float32
    slot_count = slot_table.shape[0]
    expert_count = split_count.shape[0]
    token_count, top_k = expert_ids.shape
    width = tokens.shape[1]
    hidden = w_gate.shape[2]
    capacity = max(2, (token_count * top_k + expert_count - 1) // expert_count)
    dp = lax.axis_size("dp")
    chips = slot_count // CORES
    block = -(-slot_count * capacity // dp)
    sizes = (token_count, top_k, width, capacity, block, dp, chips)

    packets = gathered(pack(tokens, expert_ids, gate_weights), chips)
    cots = gathered(cotangent, chips)
    pick, scale, rows_all, rows_own = route(slot_table, split_count, packets, sizes)

    gate_mat, up_mat, down_mat = w_gate[0], w_up[0], w_down[0]
    partial = [dot(rows_own, gate_mat, 1, 0).astype(bf16), dot(rows_own, up_mat, 1, 0).astype(bf16)]
    gate_up = reduced(jnp.concatenate(partial, axis=1), dp)
    back_all, back_own = backward_rows(pick, scale, cots)
    upstream = reduced(dot(back_own, down_mat, 1, 1).astype(bf16), dp)
    gate_pre, up_pre = gate_up[:, :hidden], gate_up[:, hidden:]
    sigma = jax.nn.sigmoid(gate_pre)
    hidden_act = gate_pre * sigma * up_pre
    gate_back = upstream * up_pre * sigma * (1.0 + gate_pre * (1.0 - sigma))
    up_back = upstream * gate_pre * sigma
    shard = jnp.concatenate([hidden_act, gate_back, up_back], axis=1).astype(bf16)
    own = spread_out(shard, dp)
    far_shard = to_chip(shard, chips // 2)

    slot_out = scale[:, 1:2] * dot(own[:, :hidden], down_mat, 1, 0)
    slot_dx = dot(own[:, hidden : 2 * hidden], gate_mat, 1, 1)
    slot_dx = slot_dx + dot(own[:, 2 * hidden :], up_mat, 1, 1)
    result = jnp.concatenate([slot_out.astype(bf16), slot_dx.astype(bf16)], axis=1)
    home = dot(pick, result, 0, 0).astype(bf16)
    home = home.reshape(CORES, chips, token_count, 2 * width)
    other = to_sibling(home[1])
    home = home[0].astype(f32) + other.astype(f32)
    total = home[0]
    for step in range(1, chips):
        total = total + to_chip(home[chips - step].astype(bf16), step).astype(f32)
    total = total.astype(bf16)

    shard = shard + scale[:block, 2:3].astype(bf16) * far_shard
    merged = spread_out(shard, dp)
    gate_grad = dot(rows_all, merged[:, hidden : 2 * hidden], 0, 0).astype(bf16)
    up_grad = dot(rows_all, merged[:, 2 * hidden :], 0, 0).astype(bf16)
    down_grad = dot(merged[:, :hidden], back_all, 0, 0).astype(bf16)
    return (total[:, :width], total[:, width:], gate_grad[None], up_grad[None], down_grad[None])


def reduced(partial, count):
    blocks = partial.reshape(count, -1, partial.shape[1])
    total = blocks[0].astype(jnp.float32)
    for step in range(1, count):
        total = total + to_peer(blocks[step], step).astype(jnp.float32)
    return total


def spread_out(value, count):
    blocks = [value]
    for step in range(1, count):
        blocks.append(from_peer(value, step))
    return jnp.concatenate(blocks)


def solution(mesh):
    return jax.shard_map(
        on_device,
        mesh=mesh,
        in_specs=(
            P("expert", "dp"),
            P("expert", "dp"),
            P("expert", None),
            P("expert", None),
            P(),
            P(),
            P("expert", "dp", None),
            P("expert", "dp", None),
            P("expert", None, "dp"),
        ),
        out_specs=(
            P("expert", "dp"),
            P("expert", "dp"),
            P("expert", "dp", None),
            P("expert", "dp", None),
            P("expert", None, "dp"),
        ),
        check_vma=False,
    )
```

time: 92.1 us -> 78.1 us (0.85)
  other arithmetic: 15 us -> 0.58 us
  starting transfers between devices: 28.4 us -> 31 us
  waiting for transfers between devices: 32.1 us -> 30 us
  Pallas kernels: 0 us -> 1.88 us
  between operations: 2.31 us -> 0.89 us
    ppermute x7 -> x10, waiting for transfers between devices: 16.8 us -> 23.2 us  [to_chip(): return lax.ppermute(value, 'expert', pairs)]
    ppermute x3 -> x6, waiting for transfers between devices: 8.38 us -> 3.52 us  [to_peer(): lax.ppermute(value, 'dp', [(i, peer(i, step, count)) for i in range(count)])]
    another operation x9 -> x2, other arithmetic: 4.25 us -> 0.23 us
    eq x2 -> x0, other arithmetic: 3.85 us -> none  [the longest x1 3.81 us: rows_of(): taken = jnp.where(source < split, lower, upper) == slot]
    ppermute x6, waiting for transfers between devices: 6.87 us -> 3.22 us  [from_peer(): lax.ppermute(value, 'dp', [(peer(i, step, count), i) for i in range(count)])]
    ppermute x3 -> x6, starting transfers between devices: 3.55 us -> 7.11 us  [to_peer(): lax.ppermute(value, 'dp', [(i, peer(i, step, count)) for i in range(count)])]
    ppermute x7 -> x10, starting transfers between devices: 17.6 us -> 14.7 us  [to_chip(): return lax.ppermute(value, 'expert', pairs)]
    reduce_sum x4 -> x0, other arithmetic: 2.86 us -> none  [the longest x1 1.95 us: rows_of(): split = jnp.sum(jnp.where(expert_iota == expert, split_count, 0))]
  transfers between devices with their start and end apart: 18 -> 31, of which waited for: 12 -> 14; matrix products, arithmetic and copies ran while one was open for 18% -> 12% of each run, Pallas kernels for 0% -> 2%
where the time goes in v2:
time: 78.1 us; the launch traced here: 77.9 us
  starting transfers between devices  31 us (40%)
  waiting for transfers between devices  30 us (38%)
  matrix products  8.78 us (11%)
  local copies, waits for them, and re-layouts  4.79 us (6%)
  Pallas kernels  1.88 us (2%)
  between operations  0.89 us (1%)
    ppermute x10, waiting for transfers between devices, to_chip(): return lax.ppermute(value, 'expert', pairs)  23.2 us
    ppermute x10, starting transfers between devices, to_chip(): return lax.ppermute(value, 'expert', pairs)  14.7 us
    dot_general x10, matrix products, dot(): lax.dot_general(left, right, (((left_dim,), (right_dim,)), ((), ())), pre...  8.78 us
    ppermute x6, starting transfers between devices, to_peer(): lax.ppermute(value, 'dp', [(i, peer(i, step, count)) for i in range(count)])  7.11 us
    ppermute x6, starting transfers between devices, from_peer(): lax.ppermute(value, 'dp', [(peer(i, step, count), i) for i in range(count)])  7.11 us
    unnamed x18, local copies, waits for them, and re-layouts  3.65 us
    ppermute x6, waiting for transfers between devices, to_peer(): lax.ppermute(value, 'dp', [(i, peer(i, step, count)) for i in range(count)])  3.52 us
    ppermute x6, waiting for transfers between devices, from_peer(): lax.ppermute(value, 'dp', [(peer(i, step, count), i) for i in range(count)])  3.22 us
  transfers between devices with their start and end apart: 31, of which 14 were waited for; matrix products, arithmetic and copies ran while one was open for 12% of the time, Pallas kernels for 2%

profile of v2, /device:TPU:0, one launch (start us, length us, event | category | flops | bytes accessed | tf_op | source)
XLA Modules:
  0.0 77.9 jit_solution(8534642552091529563)
XLA Ops:
  0.7 0.9 %copy-done.2 = bf16[32,1024]{1,0:T(8,128)(2,1)S(1)} copy-done((bf16[32,1024]{1,0:T(8,128)(2,1)S(1)}, bf16[32,1024]{1,0:T(8,128)(2,1)}, u32[]{:S(2)}) %copy-start.2) | copy-done | bytes 65560
  1.6 0.7 copy-done.3
  2.3 0.7 copy-done.4
  3.0 0.1 shard_map.128.refs_0_
  3.1 5.1 %collective-permute-start.2 = (bf16[32,1152]{1,0:T(8,128)(2,1)S(1)}, bf16[32,1152]{1,0:T(8,128)(2,1)S(1)}, u32[]{:S(2)}, u32[]{:S(2)}) collective-permute-start(bf16[32,1152]{1,0:T(8,128)(2,1)S(1)} %shard_map.128.refs_0_), channel_id=1, source_target_pairs={{0,6},{1,7},{2,0},{3,1},{4,2},{5,3},{6,4},{7,5},{8,14},{9,15},{10,... | collective-permute-start | bytes 221192 | tf_op jit(solution)/shard_map/ppermute | solution.py:34
  8.1 1.0 %collective-permute-start = (bf16[32,1152]{1,0:T(8,128)(2,1)S(1)}, bf16[32,1152]{1,0:T(8,128)(2,1)S(1)}, u32[]{:S(2)}, u32[]{:S(2)}) collective-permute-start(bf16[32,1152]{1,0:T(8,128)(2,1)S(1)} %shard_map.128.refs_0_), channel_id=1, source_target_pairs={{0,2},{1,3},{2,4},{3,5},{4,6},{5,7},{6,0},{7,1},{8,10},{9,11},{10,... | collective-permute-start | bytes 221192 | tf_op jit(solution)/shard_map/ppermute | solution.py:34
  9.1 2.8 %collective-permute-start.12 = (bf16[32,1024]{1,0:T(8,128)(2,1)}, bf16[32,1024]{1,0:T(8,128)(2,1)S(1)}, u32[]{:S(2)}, u32[]{:S(2)}) collective-permute-start(bf16[32,1024]{1,0:T(8,128)(2,1)} %refs_0_.1), channel_id=1, source_target_pairs={{0,6},{1,7},{2,0},{3,1},{4,2},{5,3},{6,4},{7,5},{8,14},{9,15},{10,... | collective-permute-start | bytes 196616 | tf_op jit(solution)/shard_map/ppermute | solution.py:34
  12.0 1.1 %collective-permute-start.11 = (bf16[32,1024]{1,0:T(8,128)(2,1)}, bf16[32,1024]{1,0:T(8,128)(2,1)S(1)}, u32[]{:S(2)}, u32[]{:S(2)}) collective-permute-start(bf16[32,1024]{1,0:T(8,128)(2,1)} %refs_0_.1), channel_id=1, source_target_pairs={{0,4},{1,5},{2,6},{3,7},{4,0},{5,1},{6,2},{7,3},{8,12},{9,13},{10,... | collective-permute-start | bytes 196616 | tf_op jit(solution)/shard_map/ppermute | solution.py:34
  13.1 2.9 %collective-permute-done.12.refs_3_ = bf16[32,1024]{1,0:T(8,128)(2,1)S(1)} collective-permute-done((bf16[32,1024]{1,0:T(8,128)(2,1)}, bf16[32,1024]{1,0:T(8,128)(2,1)S(1)}, u32[]{:S(2)}, u32[]{:S(2)}) %collective-permute-start.12) | collective-permute-done | bytes 65568 | tf_op jit(solution)/shard_map/ppermute | solution.py:34
  16.0 0.5 collective-permute-start.6
  16.5 0.2 collective-permute-done.1.refs_2_
  16.8 0.5 collective-permute-start.4
  17.3 2.1 %collective-permute-done.11.refs_2_ = bf16[32,1024]{1,0:T(8,128)(2,1)S(1)} collective-permute-done((bf16[32,1024]{1,0:T(8,128)(2,1)}, bf16[32,1024]{1,0:T(8,128)(2,1)S(1)}, u32[]{:S(2)}, u32[]{:S(2)}) %collective-permute-start.11) | collective-permute-done | bytes 65568 | tf_op jit(solution)/shard_map/ppermute | solution.py:34
  19.4 0.4 collective-permute-start.10
  19.8 5.9 %collective-permute-done.10.refs_1_ = bf16[32,1024]{1,0:T(8,128)(2,1)S(1)} collective-permute-done((bf16[32,1024]{1,0:T(8,128)(2,1)}, bf16[32,1024]{1,0:T(8,128)(2,1)S(1)}, u32[]{:S(2)}, u32[]{:S(2)}) %collective-permute-start.10) | collective-permute-done | bytes 65568 | tf_op jit(solution)/shard_map/ppermute | solution.py:34
  25.7 0.5 collective-permute-start.16
  26.3 0.4 collective-permute-start.14
  26.7 0.7 copy-done.5
  27.4 0.7 copy-done.6
  28.0 1.6 %shard_map.129 = (bf16[128,256]{1,0:T(8,128)(2,1)S(1)}, f32[128,128]{1,0:T(8,128)S(1)}, bf16[128,1024]{1,0:T(8,128)(2,1)S(1)}, bf16[128,1024]{1,0:T(8,128)(2,1)S(1)}) custom-call(s32[8]{0:T(128)S(1)} %copy-done.5, s32[6]{0:T(128)S(1)} %copy-done.6, bf16[32,1152]{1,0:T(8,128)(2,1)S(1)} %shard_map.128.refs_0_, ...), custom_call_target="tpu_custom_call" | custom-call | flops 67108864 | bytes 1048576 | tf_op jit(solution)/shard_map/pallas_call | solution.py:161
  29.6 0.4 fusion.24
  30.0 0.4 fusion.21
  30.4 1.6 %collective-permute-start.7 = (bf16[32,1536]{1,0:T(8,128)(2,1)S(1)}, bf16[32,1536]{1,0:T(8,128)(2,1)S(1)}, u32[]{:S(2)}, u32[]{:S(2)}) collective-permute-start(bf16[32,1536]{1,0:T(8,128)(2,1)S(1)} %get-tuple-element.26), channel_id=1, source_target_pairs={{0,8},{8,0},{16,24},{24,16},{1,9},{9,1},{17,25},{25,17},{2,10},{10... | collective-permute-start | bytes 294920 | tf_op jit(solution)/shard_map/ppermute | solution.py:23
  32.0 1.5 %collective-permute-start.9 = (bf16[32,1536]{1,0:T(8,128)(2,1)S(1)}, bf16[32,1536]{1,0:T(8,128)(2,1)S(1)}, u32[]{:S(2)}, u32[]{:S(2)}) collective-permute-start(bf16[32,1536]{1,0:T(8,128)(2,1)S(1)} %get-tuple-element.27), channel_id=1, source_target_pairs={{0,24},{8,16},{16,8},{24,0},{1,25},{9,17},{17,9},{25,1},{2,26},{10... | collective-permute-start | bytes 294920 | tf_op jit(solution)/shard_map/ppermute | solution.py:23
  33.5 0.5 collective-permute-start.8
  34.0 0.2 shard_map.130
  34.3 0.7 fusion.27
  35.0 1.6 %collective-permute-start.17 = (bf16[32,768]{1,0:T(8,128)(2,1)S(1)}, bf16[32,768]{1,0:T(8,128)(2,1)S(1)}, u32[]{:S(2)}, u32[]{:S(2)}) collective-permute-start(bf16[32,768]{1,0:T(8,128)(2,1)S(1)} %get-tuple-element.30), channel_id=1, source_target_pairs={{0,8},{8,0},{16,24},{24,16},{1,9},{9,1},{17,25},{25,17},{2,10},{10... | collective-permute-start | bytes 147464 | tf_op jit(solution)/shard_map/ppermute | solution.py:23
  36.5 1.5 %collective-permute-start.19 = (bf16[32,768]{1,0:T(8,128)(2,1)S(1)}, bf16[32,768]{1,0:T(8,128)(2,1)S(1)}, u32[]{:S(2)}, u32[]{:S(2)}) collective-permute-start(bf16[32,768]{1,0:T(8,128)(2,1)S(1)} %get-tuple-element.31), channel_id=1, source_target_pairs={{0,24},{8,16},{16,8},{24,0},{1,25},{9,17},{17,9},{25,1},{2,26},{10... | collective-permute-start | bytes 147464 | tf_op jit(solution)/shard_map/ppermute | solution.py:23
  38.0 0.5 collective-permute-start.18
  38.5 0.3 collective-permute-done.9
  38.9 1.9 %collective-permute-done.8 = bf16[32,1536]{1,0:T(8,128)(2,1)S(1)} collective-permute-done((bf16[32,1536]{1,0:T(8,128)(2,1)S(1)}, bf16[32,1536]{1,0:T(8,128)(2,1)S(1)}, u32[]{:S(2)}, u32[]{:S(2)}) %collective-permute-start.8) | collective-permute-done | bytes 98336 | tf_op jit(solution)/shard_map/ppermute | solution.py:23
  40.8 0.7 collective-permute-done.19
  41.5 0.6 collective-permute-done.18
  42.1 0.1 multiply_convert_fusion.2
  42.2 0.1 collective-permute-start.27
  42.3 0.2 fusion.50
  42.5 0.2 slice_reduce_fusion
  42.6 1.5 %collective-permute-start.22 = (bf16[32,2304]{1,0:T(8,128)(2,1)S(1)}, bf16[32,2304]{1,0:T(8,128)(2,1)S(1)}, u32[]{:S(2)}, u32[]{:S(2)}) collective-permute-start(bf16[32,2304]{1,0:T(8,128)(2,1)S(1)} %pad_maximum_fusion.2), channel_id=1, source_target_pairs={{24,0},{16,8},{8,16},{0,24},{25,1},{17,9},{9,17},{1,25},{26,2},{18... | collective-permute-start | bytes 442376 | tf_op jit(solution)/shard_map/ppermute | solution.py:28
  44.1 1.5 %collective-permute-start.21 = (bf16[32,2304]{1,0:T(8,128)(2,1)S(1)}, bf16[32,2304]{1,0:T(8,128)(2,1)S(1)}, u32[]{:S(2)}, u32[]{:S(2)}) collective-permute-start(bf16[32,2304]{1,0:T(8,128)(2,1)S(1)} %pad_maximum_fusion.2), channel_id=1, source_target_pairs={{16,0},{24,8},{0,16},{8,24},{17,1},{25,9},{1,17},{9,25},{18,2},{26... | collective-permute-start | bytes 442376 | tf_op jit(solution)/shard_map/ppermute | solution.py:28
  45.7 0.5 collective-permute-start.20
  46.2 2.8 %collective-permute-done.27 = bf16[32,2304]{1,0:T(8,128)(2,1)S(1)} collective-permute-done((bf16[32,2304]{1,0:T(8,128)(2,1)S(1)}, bf16[32,2304]{1,0:T(8,128)(2,1)S(1)}, u32[]{:S(2)}, u32[]{:S(2)}) %collective-permute-start.27) | collective-permute-done | bytes 147488 | tf_op jit(solution)/shard_map/ppermute | solution.py:34
  49.0 0.1 multiply_add_fusion
  49.2 1.6 %collective-permute-start.30 = (bf16[32,2304]{1,0:T(8,128)(2,1)S(1)}, bf16[32,2304]{1,0:T(8,128)(2,1)S(1)}, u32[]{:S(2)}, u32[]{:S(2)}) collective-permute-start(bf16[32,2304]{1,0:T(8,128)(2,1)S(1)} %multiply_add_fusion), channel_id=1, source_target_pairs={{24,0},{16,8},{8,16},{0,24},{25,1},{17,9},{9,17},{1,25},{26,2},{18... | collective-permute-start | bytes 442376 | tf_op jit(solution)/shard_map/ppermute | solution.py:28
  50.7 1.9 %collective-permute-start.29 = (bf16[32,2304]{1,0:T(8,128)(2,1)S(1)}, bf16[32,2304]{1,0:T(8,128)(2,1)S(1)}, u32[]{:S(2)}, u32[]{:S(2)}) collective-permute-start(bf16[32,2304]{1,0:T(8,128)(2,1)S(1)} %multiply_add_fusion), channel_id=1, source_target_pairs={{16,0},{24,8},{0,16},{8,24},{17,1},{25,9},{1,17},{9,25},{18,2},{26... | collective-permute-start | bytes 442376 | tf_op jit(solution)/shard_map/ppermute | solution.py:28
  52.8 0.6 fusion.4
  53.4 0.4 multiply_convert_fusion
  53.8 0.6 fusion.18
  54.5 0.5 convolution_convert_fusion
  54.9 0.1 fusion.53
  55.0 0.1 collective-permute-start.23
  55.1 1.3 %collective-permute-done.30 = bf16[32,2304]{1,0:T(8,128)(2,1)S(1)} collective-permute-done((bf16[32,2304]{1,0:T(8,128)(2,1)S(1)}, bf16[32,2304]{1,0:T(8,128)(2,1)S(1)}, u32[]{:S(2)}, u32[]{:S(2)}) %collective-permute-start.30) | collective-permute-done | bytes 147488 | tf_op jit(solution)/shard_map/ppermute | solution.py:28
  56.4 1.9 %collective-permute-done.29 = bf16[32,2304]{1,0:T(8,128)(2,1)S(1)} collective-permute-done((bf16[32,2304]{1,0:T(8,128)(2,1)S(1)}, bf16[32,2304]{1,0:T(8,128)(2,1)S(1)}, u32[]{:S(2)}, u32[]{:S(2)}) %collective-permute-start.29) | collective-permute-done | bytes 147488 | tf_op jit(solution)/shard_map/ppermute | solution.py:28
  58.4 1.7 %fusion.13 = bf16[1,1024,768]{2,1,0:T(8,128)(2,1)} fusion(bf16[128,1024]{1,0:T(8,128)(2,1)S(1)} %get-tuple-element.15, bf16[128,2304]{1,0:T(8,128)(2,1)S(1)} %pad_maximum_fusion.1), kind=kOutput, calls=%fused_computation.17 | convolution fusion | flops 202113024 | bytes 2031616 | tf_op jit(solution)/shard_map/dot_general | solution.py:43
  60.1 1.7 %fusion.12 = bf16[1,1024,768]{2,1,0:T(8,128)(2,1)} fusion(bf16[128,1024]{1,0:T(8,128)(2,1)S(1)} %get-tuple-element.15, bf16[128,2304]{1,0:T(8,128)(2,1)S(1)} %pad_maximum_fusion.1), kind=kOutput, calls=%fused_computation.16 | convolution fusion | flops 202113024 | bytes 2031616 | tf_op jit(solution)/shard_map/dot_general | solution.py:43
  61.9 0.1 fusion.52
  62.0 0.8 %collective-permute-start.24 = (bf16[32,2048]{1,0:T(8,128)(2,1)S(1)}, bf16[32,2048]{1,0:T(8,128)(2,1)S(1)}, u32[]{:S(2)}, u32[]{:S(2)}) collective-permute-start(bf16[32,2048]{1,0:T(8,128)(2,1)S(1)} %get-tuple-element.23), channel_id=1, source_target_pairs={{0,2},{1,3},{2,4},{3,5},{4,6},{5,7},{6,0},{7,1},{8,10},{9,11},{10,... | collective-permute-start | bytes 393224 | tf_op jit(solution)/shard_map/ppermute | solution.py:34
  62.8 3.1 %collective-permute-start.26 = (bf16[32,2048]{1,0:T(8,128)(2,1)S(1)}, bf16[32,2048]{1,0:T(8,128)(2,1)S(1)}, u32[]{:S(2)}, u32[]{:S(2)}) collective-permute-start(bf16[32,2048]{1,0:T(8,128)(2,1)S(1)} %get-tuple-element.24), channel_id=1, source_target_pairs={{0,6},{1,7},{2,0},{3,1},{4,2},{5,3},{6,4},{7,5},{8,14},{9,15},{10,... | collective-permute-start | bytes 393224 | tf_op jit(solution)/shard_map/ppermute | solution.py:34
  65.9 0.3 collective-permute-start.25
  66.3 1.7 %fusion.14 = bf16[1,768,1024]{2,1,0:T(8,128)(2,1)} fusion(bf16[128,1024]{1,0:T(8,128)(2,1)S(1)} %get-tuple-element.16, bf16[128,2304]{1,0:T(8,128)(2,1)S(1)} %pad_maximum_fusion.1), kind=kOutput, calls=%fused_computation.18 | convolution fusion | flops 202113024 | bytes 2031616 | tf_op jit(solution)/shard_map/dot_general | solution.py:43
  68.0 2.3 %collective-permute-done.24 = bf16[32,2048]{1,0:T(8,128)(2,1)S(1)} collective-permute-done((bf16[32,2048]{1,0:T(8,128)(2,1)S(1)}, bf16[32,2048]{1,0:T(8,128)(2,1)S(1)}, u32[]{:S(2)}, u32[]{:S(2)}) %collective-permute-start.24) | collective-permute-done | bytes 131104 | tf_op jit(solution)/shard_map/ppermute | solution.py:34
  70.3 0.3 collective-permute-done.26
  70.6 6.6 %collective-permute-done.25 = bf16[32,2048]{1,0:T(8,128)(2,1)S(1)} collective-permute-done((bf16[32,2048]{1,0:T(8,128)(2,1)S(1)}, bf16[32,2048]{1,0:T(8,128)(2,1)S(1)}, u32[]{:S(2)}, u32[]{:S(2)}) %collective-permute-start.25) | collective-permute-done | bytes 131104 | tf_op jit(solution)/shard_map/ppermute | solution.py:34
  77.3 0.7 fusion.55
  (44 shorter events, 0.5 us)
Async XLA Ops:
  0.6 28.9 %copy-start = (bf16[1,1024,768]{2,1,0:T(8,128)(2,1)S(1)}, bf16[1,1024,768]{2,1,0:T(8,128)(2,1)}, u32[]{:S(2)}) copy-start(bf16[1,1024,768]{2,1,0:T(8,128)(2,1)} %param.16) | copy-start | bytes 4718596
  0.6 1.0 %copy-start.2 = (bf16[32,1024]{1,0:T(8,128)(2,1)S(1)}, bf16[32,1024]{1,0:T(8,128)(2,1)}, u32[]{:S(2)}) copy-start(bf16[32,1024]{1,0:T(8,128)(2,1)} %token_ref.1) | copy-start | bytes 196612
  1.6 0.7 copy-start.3
  2.3 0.7 copy-start.4
  3.1 13.0 %collective-permute-start.2 = (bf16[32,1152]{1,0:T(8,128)(2,1)S(1)}, bf16[32,1152]{1,0:T(8,128)(2,1)S(1)}, u32[]{:S(2)}, u32[]{:S(2)}) collective-permute-start(bf16[32,1152]{1,0:T(8,128)(2,1)S(1)} %shard_map.128.refs_0_), channel_id=1, source_target_pairs={{0,6},{1,7},{2,0},{3,1},{4,2},{5,3},{6,4},{7,5},{8,14},{9,15},{10,... | collective-permute-start | bytes 221192 | tf_op jit(solution)/shard_map/ppermute | solution.py:34
  8.1 8.6 %collective-permute-start.1 = (bf16[32,1152]{1,0:T(8,128)(2,1)S(1)}, bf16[32,1152]{1,0:T(8,128)(2,1)S(1)}, u32[]{:S(2)}, u32[]{:S(2)}) collective-permute-start(bf16[32,1152]{1,0:T(8,128)(2,1)S(1)} %shard_map.128.refs_0_), channel_id=1, source_target_pairs={{0,4},{1,5},{2,6},{3,7},{4,0},{5,1},{6,2},{7,3},{8,12},{9,13},{10,... | collective-permute-start | bytes 221192 | tf_op jit(solution)/shard_map/ppermute | solution.py:34
  8.1 8.6 %collective-permute-start = (bf16[32,1152]{1,0:T(8,128)(2,1)S(1)}, bf16[32,1152]{1,0:T(8,128)(2,1)S(1)}, u32[]{:S(2)}, u32[]{:S(2)}) collective-permute-start(bf16[32,1152]{1,0:T(8,128)(2,1)S(1)} %shard_map.128.refs_0_), channel_id=1, source_target_pairs={{0,2},{1,3},{2,4},{3,5},{4,6},{5,7},{6,0},{7,1},{8,10},{9,11},{10,... | collective-permute-start | bytes 221192 | tf_op jit(solution)/shard_map/ppermute | solution.py:34
  9.1 6.9 %collective-permute-start.12 = (bf16[32,1024]{1,0:T(8,128)(2,1)}, bf16[32,1024]{1,0:T(8,128)(2,1)S(1)}, u32[]{:S(2)}, u32[]{:S(2)}) collective-permute-start(bf16[32,1024]{1,0:T(8,128)(2,1)} %refs_0_.1), channel_id=1, source_target_pairs={{0,6},{1,7},{2,0},{3,1},{4,2},{5,3},{6,4},{7,5},{8,14},{9,15},{10,... | collective-permute-start | bytes 196616 | tf_op jit(solution)/shard_map/ppermute | solution.py:34
  12.0 7.4 %collective-permute-start.11 = (bf16[32,1024]{1,0:T(8,128)(2,1)}, bf16[32,1024]{1,0:T(8,128)(2,1)S(1)}, u32[]{:S(2)}, u32[]{:S(2)}) collective-permute-start(bf16[32,1024]{1,0:T(8,128)(2,1)} %refs_0_.1), channel_id=1, source_target_pairs={{0,4},{1,5},{2,6},{3,7},{4,0},{5,1},{6,2},{7,3},{8,12},{9,13},{10,... | collective-permute-start | bytes 196616 | tf_op jit(solution)/shard_map/ppermute | solution.py:34
  16.0 9.6 %collective-permute-start.3 = (bf16[32,1152]{1,0:T(8,128)(2,1)S(1)}, bf16[32,1152]{1,0:T(8,128)(2,1)S(1)}, u32[]{:S(2)}, u32[]{:S(2)}) collective-permute-start(bf16[32,1152]{1,0:T(8,128)(2,1)S(1)} %shard_map.128.refs_0_), channel_id=1, source_target_pairs={{0,1},{1,0},{2,3},{3,2},{4,5},{5,4},{6,7},{7,6},{8,9},{9,8},{10,11... | collective-permute-start | bytes 221192 | tf_op jit(solution)/shard_map/ppermute | solution.py:39
  16.0 10.1 %collective-permute-start.6 = (bf16[32,1152]{1,0:T(8,128)(2,1)S(1)}, bf16[32,1152]{1,0:T(8,128)(2,1)S(1)}, u32[]{:S(2)}, u32[]{:S(2)}) collective-permute-start(bf16[32,1152]{1,0:T(8,128)(2,1)S(1)} %collective-permute-done.2.refs_3_), channel_id=1, source_target_pairs={{0,1},{1,0},{2,3},{3,2},{4,5},{5,4},{6,7},{7,6},{8,9},{9,8},{10,11... | collective-permute-start | bytes 221192 | tf_op jit(solution)/shard_map/ppermute | solution.py:39
  16.8 9.5 %collective-permute-start.5 = (bf16[32,1152]{1,0:T(8,128)(2,1)S(1)}, bf16[32,1152]{1,0:T(8,128)(2,1)S(1)}, u32[]{:S(2)}, u32[]{:S(2)}) collective-permute-start(bf16[32,1152]{1,0:T(8,128)(2,1)S(1)} %collective-permute-done.1.refs_2_), channel_id=1, source_target_pairs={{0,1},{1,0},{2,3},{3,2},{4,5},{5,4},{6,7},{7,6},{8,9},{9,8},{10,11... | collective-permute-start | bytes 221192 | tf_op jit(solution)/shard_map/ppermute | solution.py:39
  16.8 9.9 %collective-permute-start.4 = (bf16[32,1152]{1,0:T(8,128)(2,1)S(1)}, bf16[32,1152]{1,0:T(8,128)(2,1)S(1)}, u32[]{:S(2)}, u32[]{:S(2)}) collective-permute-start(bf16[32,1152]{1,0:T(8,128)(2,1)S(1)} %collective-permute-done.refs_1_), channel_id=1, source_target_pairs={{0,1},{1,0},{2,3},{3,2},{4,5},{5,4},{6,7},{7,6},{8,9},{9,8},{10,11... | collective-permute-start | bytes 221192 | tf_op jit(solution)/shard_map/ppermute | solution.py:39
  19.4 6.3 %collective-permute-start.10 = (bf16[32,1024]{1,0:T(8,128)(2,1)}, bf16[32,1024]{1,0:T(8,128)(2,1)S(1)}, u32[]{:S(2)}, u32[]{:S(2)}) collective-permute-start(bf16[32,1024]{1,0:T(8,128)(2,1)} %refs_0_.1), channel_id=1, source_target_pairs={{0,2},{1,3},{2,4},{3,5},{4,6},{5,7},{6,0},{7,1},{8,10},{9,11},{10,... | collective-permute-start | bytes 196616 | tf_op jit(solution)/shard_map/ppermute | solution.py:34
  25.7 6.3 %collective-permute-start.13 = (bf16[32,1024]{1,0:T(8,128)(2,1)}, bf16[32,1024]{1,0:T(8,128)(2,1)S(1)}, u32[]{:S(2)}, u32[]{:S(2)}) collective-permute-start(bf16[32,1024]{1,0:T(8,128)(2,1)} %refs_0_.1), channel_id=1, source_target_pairs={{0,1},{1,0},{2,3},{3,2},{4,5},{5,4},{6,7},{7,6},{8,9},{9,8},{10,11... | collective-permute-start | bytes 196616 | tf_op jit(solution)/shard_map/ppermute | solution.py:39
  25.7 7.8 %collective-permute-start.16 = (bf16[32,1024]{1,0:T(8,128)(2,1)S(1)}, bf16[32,1024]{1,0:T(8,128)(2,1)S(1)}, u32[]{:S(2)}, u32[]{:S(2)}) collective-permute-start(bf16[32,1024]{1,0:T(8,128)(2,1)S(1)} %collective-permute-done.12.refs_3_), channel_id=1, source_target_pairs={{0,1},{1,0},{2,3},{3,2},{4,5},{5,4},{6,7},{7,6},{8,9},{9,8},{10,11... | collective-permute-start | bytes 196616 | tf_op jit(solution)/shard_map/ppermute | solution.py:39
  26.2 7.8 %collective-permute-start.15 = (bf16[32,1024]{1,0:T(8,128)(2,1)S(1)}, bf16[32,1024]{1,0:T(8,128)(2,1)S(1)}, u32[]{:S(2)}, u32[]{:S(2)}) collective-permute-start(bf16[32,1024]{1,0:T(8,128)(2,1)S(1)} %collective-permute-done.11.refs_2_), channel_id=1, source_target_pairs={{0,1},{1,0},{2,3},{3,2},{4,5},{5,4},{6,7},{7,6},{8,9},{9,8},{10,11... | collective-permute-start | bytes 196616 | tf_op jit(solution)/shard_map/ppermute | solution.py:39
  26.3 7.7 %collective-permute-start.14 = (bf16[32,1024]{1,0:T(8,128)(2,1)S(1)}, bf16[32,1024]{1,0:T(8,128)(2,1)S(1)}, u32[]{:S(2)}, u32[]{:S(2)}) collective-permute-start(bf16[32,1024]{1,0:T(8,128)(2,1)S(1)} %collective-permute-done.10.refs_1_), channel_id=1, source_target_pairs={{0,1},{1,0},{2,3},{3,2},{4,5},{5,4},{6,7},{7,6},{8,9},{9,8},{10,11... | collective-permute-start | bytes 196616 | tf_op jit(solution)/shard_map/ppermute | solution.py:39
  26.7 0.7 copy-start.5
  27.4 0.7 copy-start.6
  28.0 2.0 %copy-start.8 = (bf16[1,1024,768]{2,1,0:T(8,128)(2,1)S(1)}, bf16[1,1024,768]{2,1,0:T(8,128)(2,1)}, u32[]{:S(2)}) copy-start(bf16[1,1024,768]{2,1,0:T(8,128)(2,1)} %param.15) | copy-start | bytes 4718596
  30.0 4.0 %copy-start.1 = (bf16[32,1024]{1,0:T(8,128)(2,1)S(1)}, bf16[32,1024]{1,0:T(8,128)(2,1)}, u32[]{:S(2)}) copy-start(bf16[32,1024]{1,0:T(8,128)(2,1)} %refs_0_.1) | copy-start | bytes 196612
  30.0 4.3 %copy-start.7 = (bf16[1,768,1024]{2,1,0:T(8,128)(2,1)S(1)}, bf16[1,768,1024]{2,1,0:T(8,128)(2,1)}, u32[]{:S(2)}) copy-start(bf16[1,768,1024]{2,1,0:T(8,128)(2,1)} %param.17) | copy-start | bytes 4718596
  30.4 7.6 %collective-permute-start.7 = (bf16[32,1536]{1,0:T(8,128)(2,1)S(1)}, bf16[32,1536]{1,0:T(8,128)(2,1)S(1)}, u32[]{:S(2)}, u32[]{:S(2)}) collective-permute-start(bf16[32,1536]{1,0:T(8,128)(2,1)S(1)} %get-tuple-element.26), channel_id=1, source_target_pairs={{0,8},{8,0},{16,24},{24,16},{1,9},{9,1},{17,25},{25,17},{2,10},{10... | collective-permute-start | bytes 294920 | tf_op jit(solution)/shard_map/ppermute | solution.py:23
  32.0 6.9 %collective-permute-start.9 = (bf16[32,1536]{1,0:T(8,128)(2,1)S(1)}, bf16[32,1536]{1,0:T(8,128)(2,1)S(1)}, u32[]{:S(2)}, u32[]{:S(2)}) collective-permute-start(bf16[32,1536]{1,0:T(8,128)(2,1)S(1)} %get-tuple-element.27), channel_id=1, source_target_pairs={{0,24},{8,16},{16,8},{24,0},{1,25},{9,17},{17,9},{25,1},{2,26},{10... | collective-permute-start | bytes 294920 | tf_op jit(solution)/shard_map/ppermute | solution.py:23
  33.5 7.2 %collective-permute-start.8 = (bf16[32,1536]{1,0:T(8,128)(2,1)S(1)}, bf16[32,1536]{1,0:T(8,128)(2,1)S(1)}, u32[]{:S(2)}, u32[]{:S(2)}) collective-permute-start(bf16[32,1536]{1,0:T(8,128)(2,1)S(1)} %get-tuple-element.28), channel_id=1, source_target_pairs={{0,16},{8,24},{16,0},{24,8},{1,17},{9,25},{17,1},{25,9},{2,18},{10... | collective-permute-start | bytes 294920 | tf_op jit(solution)/shard_map/ppermute | solution.py:23
  35.0 5.8 %collective-permute-start.17 = (bf16[32,768]{1,0:T(8,128)(2,1)S(1)}, bf16[32,768]{1,0:T(8,128)(2,1)S(1)}, u32[]{:S(2)}, u32[]{:S(2)}) collective-permute-start(bf16[32,768]{1,0:T(8,128)(2,1)S(1)} %get-tuple-element.30), channel_id=1, source_target_pairs={{0,8},{8,0},{16,24},{24,16},{1,9},{9,1},{17,25},{25,17},{2,10},{10... | collective-permute-start | bytes 147464 | tf_op jit(solution)/shard_map/ppermute | solution.py:23
  36.5 5.0 %collective-permute-start.19 = (bf16[32,768]{1,0:T(8,128)(2,1)S(1)}, bf16[32,768]{1,0:T(8,128)(2,1)S(1)}, u32[]{:S(2)}, u32[]{:S(2)}) collective-permute-start(bf16[32,768]{1,0:T(8,128)(2,1)S(1)} %get-tuple-element.31), channel_id=1, source_target_pairs={{0,24},{8,16},{16,8},{24,0},{1,25},{9,17},{17,9},{25,1},{2,26},{10... | collective-permute-start | bytes 147464 | tf_op jit(solution)/shard_map/ppermute | solution.py:23
  38.0 4.1 %collective-permute-start.18 = (bf16[32,768]{1,0:T(8,128)(2,1)S(1)}, bf16[32,768]{1,0:T(8,128)(2,1)S(1)}, u32[]{:S(2)}, u32[]{:S(2)}) collective-permute-start(bf16[32,768]{1,0:T(8,128)(2,1)S(1)} %get-tuple-element.32), channel_id=1, source_target_pairs={{0,16},{8,24},{16,0},{24,8},{1,17},{9,25},{17,1},{25,9},{2,18},{10... | collective-permute-start | bytes 147464 | tf_op jit(solution)/shard_map/ppermute | solution.py:23
  42.2 6.8 %collective-permute-start.27 = (bf16[32,2304]{1,0:T(8,128)(2,1)S(1)}, bf16[32,2304]{1,0:T(8,128)(2,1)S(1)}, u32[]{:S(2)}, u32[]{:S(2)}) collective-permute-start(bf16[32,2304]{1,0:T(8,128)(2,1)S(1)} %pad_maximum_fusion.2), channel_id=1, source_target_pairs={{0,4},{1,5},{2,6},{3,7},{4,0},{5,1},{6,2},{7,3},{8,12},{9,13},{10,... | collective-permute-start | bytes 442376 | tf_op jit(solution)/shard_map/ppermute | solution.py:34
  42.6 10.0 %collective-permute-start.22 = (bf16[32,2304]{1,0:T(8,128)(2,1)S(1)}, bf16[32,2304]{1,0:T(8,128)(2,1)S(1)}, u32[]{:S(2)}, u32[]{:S(2)}) collective-permute-start(bf16[32,2304]{1,0:T(8,128)(2,1)S(1)} %pad_maximum_fusion.2), channel_id=1, source_target_pairs={{24,0},{16,8},{8,16},{0,24},{25,1},{17,9},{9,17},{1,25},{26,2},{18... | collective-permute-start | bytes 442376 | tf_op jit(solution)/shard_map/ppermute | solution.py:28
  44.1 8.6 %collective-permute-start.21 = (bf16[32,2304]{1,0:T(8,128)(2,1)S(1)}, bf16[32,2304]{1,0:T(8,128)(2,1)S(1)}, u32[]{:S(2)}, u32[]{:S(2)}) collective-permute-start(bf16[32,2304]{1,0:T(8,128)(2,1)S(1)} %pad_maximum_fusion.2), channel_id=1, source_target_pairs={{16,0},{24,8},{0,16},{8,24},{17,1},{25,9},{1,17},{9,25},{18,2},{26... | collective-permute-start | bytes 442376 | tf_op jit(solution)/shard_map/ppermute | solution.py:28
  45.7 7.1 %collective-permute-start.20 = (bf16[32,2304]{1,0:T(8,128)(2,1)S(1)}, bf16[32,2304]{1,0:T(8,128)(2,1)S(1)}, u32[]{:S(2)}, u32[]{:S(2)}) collective-permute-start(bf16[32,2304]{1,0:T(8,128)(2,1)S(1)} %pad_maximum_fusion.2), channel_id=1, source_target_pairs={{8,0},{0,8},{24,16},{16,24},{9,1},{1,9},{25,17},{17,25},{10,2},{2,... | collective-permute-start | bytes 442376 | tf_op jit(solution)/shard_map/ppermute | solution.py:28
  49.2 7.2 %collective-permute-start.30 = (bf16[32,2304]{1,0:T(8,128)(2,1)S(1)}, bf16[32,2304]{1,0:T(8,128)(2,1)S(1)}, u32[]{:S(2)}, u32[]{:S(2)}) collective-permute-start(bf16[32,2304]{1,0:T(8,128)(2,1)S(1)} %multiply_add_fusion), channel_id=1, source_target_pairs={{24,0},{16,8},{8,16},{0,24},{25,1},{17,9},{9,17},{1,25},{26,2},{18... | collective-permute-start | bytes 442376 | tf_op jit(solution)/shard_map/ppermute | solution.py:28
  50.7 7.6 %collective-permute-start.29 = (bf16[32,2304]{1,0:T(8,128)(2,1)S(1)}, bf16[32,2304]{1,0:T(8,128)(2,1)S(1)}, u32[]{:S(2)}, u32[]{:S(2)}) collective-permute-start(bf16[32,2304]{1,0:T(8,128)(2,1)S(1)} %multiply_add_fusion), channel_id=1, source_target_pairs={{16,0},{24,8},{0,16},{8,24},{17,1},{25,9},{1,17},{9,25},{18,2},{26... | collective-permute-start | bytes 442376 | tf_op jit(solution)/shard_map/ppermute | solution.py:28
  52.7 5.6 %collective-permute-start.28 = (bf16[32,2304]{1,0:T(8,128)(2,1)S(1)}, bf16[32,2304]{1,0:T(8,128)(2,1)S(1)}, u32[]{:S(2)}, u32[]{:S(2)}) collective-permute-start(bf16[32,2304]{1,0:T(8,128)(2,1)S(1)} %multiply_add_fusion), channel_id=1, source_target_pairs={{8,0},{0,8},{24,16},{16,24},{9,1},{1,9},{25,17},{17,25},{10,2},{2,... | collective-permute-start | bytes 442376 | tf_op jit(solution)/shard_map/ppermute | solution.py:28
  55.0 6.8 %collective-permute-start.23 = (bf16[4,32,2048]{2,1,0:T(8,128)(2,1)S(1)}, bf16[4,32,2048]{2,1,0:T(8,128)(2,1)S(1)}, u32[]{:S(2)}, u32[]{:S(2)}) collective-permute-start(bf16[4,32,2048]{2,1,0:T(8,128)(2,1)S(1)} %bitcast.64), channel_id=1, source_target_pairs={{0,1},{1,0},{2,3},{3,2},{4,5},{5,4},{6,7},{7,6},{8,9},{9,8},{10,11... | collective-permute-start | bytes 1572872 | tf_op jit(solution)/shard_map/ppermute | solution.py:39
  62.0 8.2 %collective-permute-start.24 = (bf16[32,2048]{1,0:T(8,128)(2,1)S(1)}, bf16[32,2048]{1,0:T(8,128)(2,1)S(1)}, u32[]{:S(2)}, u32[]{:S(2)}) collective-permute-start(bf16[32,2048]{1,0:T(8,128)(2,1)S(1)} %get-tuple-element.23), channel_id=1, source_target_pairs={{0,2},{1,3},{2,4},{3,5},{4,6},{5,7},{6,0},{7,1},{8,10},{9,11},{10,... | collective-permute-start | bytes 393224 | tf_op jit(solution)/shard_map/ppermute | solution.py:34
  62.8 7.8 %collective-permute-start.26 = (bf16[32,2048]{1,0:T(8,128)(2,1)S(1)}, bf16[32,2048]{1,0:T(8,128)(2,1)S(1)}, u32[]{:S(2)}, u32[]{:S(2)}) collective-permute-start(bf16[32,2048]{1,0:T(8,128)(2,1)S(1)} %get-tuple-element.24), channel_id=1, source_target_pairs={{0,6},{1,7},{2,0},{3,1},{4,2},{5,3},{6,4},{7,5},{8,14},{9,15},{10,... | collective-permute-start | bytes 393224 | tf_op jit(solution)/shard_map/ppermute | solution.py:34
  65.9 11.3 %collective-permute-start.25 = (bf16[32,2048]{1,0:T(8,128)(2,1)S(1)}, bf16[32,2048]{1,0:T(8,128)(2,1)S(1)}, u32[]{:S(2)}, u32[]{:S(2)}) collective-permute-start(bf16[32,2048]{1,0:T(8,128)(2,1)S(1)} %get-tuple-element.25), channel_id=1, source_target_pairs={{0,4},{1,5},{2,6},{3,7},{4,0},{5,1},{6,2},{7,3},{8,12},{9,13},{10,... | collective-permute-start | bytes 393224 | tf_op jit(solution)/shard_map/ppermute | solution.py:34
